TPU v7x, 256 devices: a whole 4x4x8 slice. The times are simulated.
256 devices in a mesh: dp: 2 (over core), space: 128 (over x, z, y).
Axes of the slice: x: 4, y: 4, z: 8, core: 2. Of those that a mesh axis runs over, the one named last changes fastest.
Arguments:
- feats: bfloat16 [262144, 64], P(('dp', 'space')), parts along dimension 0, may hold values from -6 to 6
- w_conv: bfloat16 [1728, 64], replicated, may hold values from -0.1875 to 0.1875
- w_down: bfloat16 [512, 128], replicated, may hold values from -0.375 to 0.375
- neighbors: int32 [27, 262144], P(None, ('dp', 'space')), parts along dimension 1, may hold values from 0 to 3072, as said below
- parent: int32 [262144], P(('dp', 'space')), parts along dimension 0, may hold values from 0 to 32767, as said below
- octant: int32 [262144], P(('dp', 'space')), parts along dimension 0, may hold values from 0 to 7, as said below
- grad_out: bfloat16 [65536, 128], P(('dp', 'space')), parts along dimension 0, may hold values from -6 to 6
Outputs:
- coarse_out: bfloat16 [65536, 128], P(('dp', 'space')), parts along dimension 0
- grad_feats: bfloat16 [262144, 64], P(('dp', 'space')), parts along dimension 0
- grad_conv: float32 [3456, 64], P('dp'), parts along dimension 0
- grad_down: float32 [1024, 128], P('dp'), parts along dimension 0
There are 2 independent parts, one for each index of `dp`. A program takes and returns all parts, laid end to end along the dimension named above; an argument that names none is the same for every part. Nothing has to cross between parts.
Inputs may be any that keep to these rules, and one draw needn't show every extreme that they name: For v in aligned block j of 1024 rows, neighbors[k, v] = r < 3072 names the fine voxel (j - 1) * 1024 + r at offset (k // 9 - 1, k // 3 % 3 - 1, k % 3 - 1) from v, and 3072 marks an empty cell; neighbors[13, v] = 1024 + v % 1024; a named row of block j - 1 is among its last 512 rows and a named row of block j + 1 among its first 512 rows; rows of block 0 never name block -1 and rows of the last block never name the block after it; the table is symmetric: the voxel named by neighbors[k, v] names v at offset 26 - k. A fine voxel in aligned block j of 1024 rows has its parent in coarse block j or j - 1 of 256 rows, block 127 standing for j - 1 when j = 0; no two fine voxels share both parent and octant. `octant`: the corner of the parent's 2x2x2 cell that the fine voxel occupies.
All inputs are finite; a program needn't handle non-finite values.
Results may differ from a plain program's by a relative error of at most 0.0049.
Values may be sent and summed in bfloat16 or wider, within the bound.
A program may use at most 64 MiB of HBM per device.

v0:
```python
import math

import jax
import jax.numpy as jnp
from jax import lax
from jax.sharding import PartitionSpec as P


def with_halo(cells, sides, width):
    for axis, dim in sides:
        count = lax.axis_size(axis)
        ends = count - 1
        head = lax.slice_in_dim(cells, 0, width, axis=dim)
        tail = lax.slice_in_dim(cells, cells.shape[dim] - width, cells.shape[dim], axis=dim)
        cells = jnp.concatenate(
            [
                lax.ppermute(tail, axis, [(i, (i + 1) % count) for i in range(ends)]),
                cells,
                lax.ppermute(head, axis, [((i + 1) % count, i) for i in range(ends)]),
            ],
            axis=dim,
        )
    return cells


def shifted(value, axis, steps):
    count = lax.axis_size(axis)
    pairs = [(source, (source + steps) % count) for source in range(count)]
    return lax.ppermute(value, axis, pairs)


def transposed_dot(left, right):
    return lax.dot_general(
        left, right, (((0,), (0,)), ((), ())), preferred_element_type=jnp.float32
    )


def per_device(feats, w_conv, w_down, neighbors, parent, octant, grad_out):
    row_count, feat_width = feats.shape
    space_size = lax.axis_size("space")
    place = lax.axis_index("space")
    voxels = row_count * space_size
    coarse_count = grad_out.shape[0]
    zero_row = jnp.zeros((1, feat_width), jnp.bfloat16)
    rimmed = with_halo(feats, (("space", 0),), row_count)
    lookup = jnp.concatenate([rimmed, zero_row], axis=0)
    local_ids = jnp.where(
        neighbors == 3 * row_count, 2 * row_count + row_count, neighbors - (row_count - row_count)
    )
    gathered = lookup[local_ids.T].reshape(row_count, 27 * feat_width)
    preact = jnp.dot(gathered, w_conv, preferred_element_type=jnp.float32)
    middle = (feats.astype(jnp.float32) + jax.nn.silu(preact)).astype(jnp.bfloat16)
    slot_hot = octant[:, None] == jnp.arange(8, dtype=jnp.int32)[None, :]
    spread = jnp.where(
        slot_hot[:, :, None], middle[:, None, :], jnp.zeros((), jnp.bfloat16)
    ).reshape(row_count, 8 * feat_width)
    own_start = place * coarse_count
    prev_start = (place - 1) % space_size * coarse_count
    inside = (parent >= own_start) & (parent < own_start + coarse_count)
    coarse_ids = jnp.where(inside, parent - own_start + coarse_count, parent - prev_start)
    parent_hot = (
        coarse_ids[:, None] == jnp.arange(2 * coarse_count, dtype=jnp.int32)[None, :]
    ).astype(jnp.bfloat16)
    children = transposed_dot(parent_hot, spread).astype(jnp.bfloat16)
    coarse_sums = jnp.dot(children, w_down, preferred_element_type=jnp.float32)
    incoming = shifted(coarse_sums[:coarse_count].astype(jnp.bfloat16), "space", -1).astype(
        jnp.float32
    )
    coarse_out = (coarse_sums[coarse_count:] + incoming).astype(jnp.bfloat16)
    from_before = shifted(grad_out, "space", 1)
    coarse_lookup = jnp.concatenate([from_before, grad_out], axis=0)
    parent_grads = jnp.dot(parent_hot, coarse_lookup, preferred_element_type=jnp.float32).astype(
        jnp.bfloat16
    )
    back_all = jnp.dot(parent_grads, w_down.T, preferred_element_type=jnp.float32)
    back_mid = jnp.sum(
        jnp.where(
            slot_hot[:, :, None], back_all.reshape(row_count, 8, feat_width), jnp.float32(0.0)
        ),
        axis=1,
    )
    down_local = transposed_dot(children, coarse_lookup)
    sigmoid_pre = jax.nn.sigmoid(preact)
    grad_pre = (back_mid * sigmoid_pre * (1.0 + preact * (1.0 - sigmoid_pre))).astype(jnp.bfloat16)
    conv_local = transposed_dot(gathered, grad_pre)
    conv_total, down_total = lax.psum((conv_local, down_local), "space")
    grad_scale = 1.0 / math.sqrt(voxels)
    grad_conv = conv_total * grad_scale
    grad_down = down_total * grad_scale
    grad_rimmed = with_halo(grad_pre, (("space", 0),), row_count)
    grad_lookup = jnp.concatenate([grad_rimmed, zero_row], axis=0)
    grad_gathered = grad_lookup[local_ids.T].reshape(row_count, 27 * feat_width)
    flipped = (
        w_conv.reshape(27, feat_width, feat_width)[::-1]
        .transpose(0, 2, 1)
        .reshape(27 * feat_width, feat_width)
    )
    grad_feats = back_mid + jnp.dot(grad_gathered, flipped, preferred_element_type=jnp.float32)
    return (coarse_out, grad_feats.astype(jnp.bfloat16), grad_conv, grad_down)


def solution(mesh):
    in_specs = (
        P(("dp", "space"), None),
        P(),
        P(),
        P(None, ("dp", "space")),
        P(("dp", "space")),
        P(("dp", "space")),
        P(("dp", "space"), None),
    )
    out_specs = (P(("dp", "space"), None), P(("dp", "space"), None), P("dp", None), P("dp", None))
    return jax.shard_map(
        per_device, mesh=mesh, in_specs=in_specs, out_specs=out_specs, check_vma=False
    )
```

profile of v0, /device:TPU:8, one launch (start us, length us, event | category | flops | bytes accessed | tf_op | source)
XLA Modules:
  0.0 386.7 jit_solution(2754344190714112376)
XLA Ops:
  7.2 1.1 copy.18
  8.3 3.5 collective-permute-start
  11.8 3.0 collective-permute-start.1
  14.9 1.0 collective-permute-start.3
  16.6 0.9 compare_select_fusion
  18.8 1.4 reshape.49
  20.8 1.2 fusion.5
  22.3 1.5 maximum_maximum_fusion
  23.8 96.4 %gather_fusion = bf16[27648,64]{1,0:T(8,128)(2,1)} fusion(bf16[3073,64]{1,0:T(8,128)(2,1)S(1)} %maximum_maximum_fusion, s32[27648]{0:T(1024)S(1)} %broadcast_clamp_fusion), kind=kCustom, calls=%fused_computation | custom fusion | bytes 7188480 | tf_op jit(solution)/shard_map/gather | solution.py:50
  120.2 10.1 %reshape.47 = bf16[1024,1728]{1,0:T(8,128)(2,1)} reshape(bf16[27648,64]{1,0:T(8,128)(2,1)} %gather_fusion) | data formatting | bytes 7077888 | tf_op jit(solution)/shard_map/reshape | solution.py:50
  130.3 3.5 multiply_convert_fusion
  133.8 1.5 fusion.24
  135.4 1.0 convolution_convert_fusion
  136.8 7.6 %collective-permute-start.2 = (bf16[256,128]{1,0:T(8,128)(2,1)S(1)}, bf16[256,128]{1,0:T(8,128)(2,1)S(1)}, u32[]{:S(2)}, u32[]{:S(2)}) collective-permute-start(bf16[256,128]{1,0:T(8,128)(2,1)S(1)} %slice.19), channel_id=1, source_target_pairs={{0,127},{1,0},{2,1},{3,2},{4,3},{5,4},{6,5},{7,6},{8,7},{9,8},{10,... | collective-permute-start | bytes 196616 | tf_op jit(solution)/shard_map/ppermute | solution.py:29
  144.4 1.0 fusion.23
  145.5 1.9 collective-permute-start.4
  147.4 4.1 %collective-permute-start.5 = (bf16[1024,64]{0,1:T(8,128)(2,1)S(1)}, bf16[1024,64]{0,1:T(8,128)(2,1)S(1)}, u32[]{:S(2)}, u32[]{:S(2)}) collective-permute-start(bf16[1024,64]{0,1:T(8,128)(2,1)S(1)} %get-tuple-element.6), channel_id=1, source_target_pairs={{1,0},{2,1},{3,2},{4,3},{5,4},{6,5},{7,6},{8,7},{9,8},{10,9},{11,1... | collective-permute-start | bytes 393224 | tf_op jit(solution)/shard_map/ppermute | solution.py:19
  152.3 1.9 collective-permute-done.5
  154.7 96.4 %gather_fusion.1 = bf16[27648,64]{1,0:T(8,128)(2,1)} fusion(bf16[3073,64]{1,0:T(8,128)(2,1)S(1)} %copy.23, s32[27648]{0:T(1024)S(1)} %broadcast_clamp_fusion), kind=kCustom, calls=%fused_computation.1 | custom fusion | bytes 7188480 | tf_op jit(solution)/shard_map/gather | solution.py:92
  251.1 12.3 %reshape.59 = bf16[1024,27,64]{2,1,0:T(8,128)(2,1)} reshape(bf16[27648,64]{1,0:T(8,128)(2,1)} %gather_fusion.1) | data formatting | bytes 7077888 | tf_op jit(solution)/shard_map/gather | solution.py:92
  263.4 8.3 %fusion.12 = bf16[1024,64]{0,1:T(8,128)(2,1)} fusion(f32[1024,64]{0,1:T(8,128)S(1)} %select_reduce_fusion, bf16[1024,27,64]{2,1,0:T(8,128)(2,1)} %reshape.59, bf16[27,64,64]{2,0,1:T(8,128)(2,1)S(1)} %bitcast.30), kind=kOutput, calls=%fused_computation.13 | convolution fusion | flops 226623488 | bytes 4153344 | tf_op jit(solution)/shard_map/dot_general | solution.py:98
  271.7 104.6 %all-reduce.3.cloned.1.call-done = (f32[1728,64]{0,1:T(8,128)}, f32[512,128]{1,0:T(8,128)}) async-done(((f32[1728,64]{0,1:T(8,128)}, f32[512,128]{1,0:T(8,128)}), (f32[1728,64]{0,1:T(8,128)}, f32[512,128]{1,0:T(8,128)})) %all-reduce.3.cloned.1.call-update) | async-done | bytes 704528 | tf_op jit(solution)/shard_map/psum | solution.py:86
  376.3 1.8 broadcast_multiply_fusion
  378.1 1.7 broadcast_multiply_fusion.1
  (33 shorter events, 4.5 us)
Async XLA Ops:
  7.2 13.6 %copy-start = (bf16[512,128]{1,0:T(8,128)(2,1)S(1)}, bf16[512,128]{1,0:T(8,128)(2,1)}, u32[]{:S(2)}) copy-start(bf16[512,128]{1,0:T(8,128)(2,1)} %param.9) | copy-start | bytes 393220
  7.2 13.6 %copy-start.4 = (bf16[256,128]{1,0:T(8,128)(2,1)S(1)}, bf16[256,128]{1,0:T(8,128)(2,1)}, u32[]{:S(2)}) copy-start(bf16[256,128]{1,0:T(8,128)(2,1)} %param.13) | copy-start | bytes 196612
  7.2 369.1 %all-reduce.3.cloned.1.call-start = ((), (), s32[]{:S(2)}) async-start(), calls=%async_computation | async-start | bytes 1441792 | tf_op jit(solution)/shard_map/psum | solution.py:86
  8.3 13.9 %collective-permute-start = (bf16[1024,64]{1,0:T(8,128)(2,1)S(1)}, bf16[1024,64]{1,0:T(8,128)(2,1)}, u32[]{:S(2)}, u32[]{:S(2)}) collective-permute-start(bf16[1024,64]{1,0:T(8,128)(2,1)S(1)} %copy.18), channel_id=1, source_target_pairs={{0,1},{1,2},{2,3},{3,4},{4,5},{5,6},{6,7},{7,8},{8,9},{9,10},{10,1... | collective-permute-start | bytes 393224 | tf_op jit(solution)/shard_map/ppermute | solution.py:17
  11.8 10.4 %collective-permute-start.1 = (bf16[1024,64]{1,0:T(8,128)(2,1)S(1)}, bf16[1024,64]{1,0:T(8,128)(2,1)}, u32[]{:S(2)}, u32[]{:S(2)}) collective-permute-start(bf16[1024,64]{1,0:T(8,128)(2,1)S(1)} %copy.18), channel_id=1, source_target_pairs={{1,0},{2,1},{3,2},{4,3},{5,4},{6,5},{7,6},{8,7},{9,8},{10,9},{11,1... | collective-permute-start | bytes 393224 | tf_op jit(solution)/shard_map/ppermute | solution.py:19
  14.9 5.9 %collective-permute-start.3 = (bf16[256,128]{1,0:T(8,128)(2,1)}, bf16[256,128]{1,0:T(8,128)(2,1)S(1)}, u32[]{:S(2)}, u32[]{:S(2)}) collective-permute-start(bf16[256,128]{1,0:T(8,128)(2,1)} %param.13), channel_id=1, source_target_pairs={{0,1},{1,2},{2,3},{3,4},{4,5},{5,6},{6,7},{7,8},{8,9},{9,10},{10,1... | collective-permute-start | bytes 196616 | tf_op jit(solution)/shard_map/ppermute | solution.py:29
  120.2 10.1 %copy-start.2 = (bf16[1728,64]{0,1:T(8,128)(2,1)S(1)}, bf16[1728,64]{0,1:T(8,128)(2,1)}, u32[]{:S(2)}) copy-start(bf16[1728,64]{0,1:T(8,128)(2,1)} %param.8) | copy-start | bytes 663556
  120.2 10.1 %copy-start.3 = (bf16[1024,64]{0,1:T(8,128)(2,1)S(1)}, bf16[1024,64]{0,1:T(8,128)(2,1)}, u32[]{:S(2)}) copy-start(bf16[1024,64]{0,1:T(8,128)(2,1)} %param.7) | copy-start | bytes 393220
  130.3 3.5 copy-start.1
  136.8 14.7 %collective-permute-start.2 = (bf16[256,128]{1,0:T(8,128)(2,1)S(1)}, bf16[256,128]{1,0:T(8,128)(2,1)S(1)}, u32[]{:S(2)}, u32[]{:S(2)}) collective-permute-start(bf16[256,128]{1,0:T(8,128)(2,1)S(1)} %slice.19), channel_id=1, source_target_pairs={{0,127},{1,0},{2,1},{3,2},{4,3},{5,4},{6,5},{7,6},{8,7},{9,8},{10,... | collective-permute-start | bytes 196616 | tf_op jit(solution)/shard_map/ppermute | solution.py:29
  145.5 6.8 %collective-permute-start.4 = (bf16[1024,64]{0,1:T(8,128)(2,1)S(1)}, bf16[1024,64]{0,1:T(8,128)(2,1)S(1)}, u32[]{:S(2)}, u32[]{:S(2)}) collective-permute-start(bf16[1024,64]{0,1:T(8,128)(2,1)S(1)} %get-tuple-element.6), channel_id=1, source_target_pairs={{0,1},{1,2},{2,3},{3,4},{4,5},{5,6},{6,7},{7,8},{8,9},{9,10},{10,1... | collective-permute-start | bytes 393224 | tf_op jit(solution)/shard_map/ppermute | solution.py:17
  147.4 6.9 %collective-permute-start.5 = (bf16[1024,64]{0,1:T(8,128)(2,1)S(1)}, bf16[1024,64]{0,1:T(8,128)(2,1)S(1)}, u32[]{:S(2)}, u32[]{:S(2)}) collective-permute-start(bf16[1024,64]{0,1:T(8,128)(2,1)S(1)} %get-tuple-element.6), channel_id=1, source_target_pairs={{1,0},{2,1},{3,2},{4,3},{5,4},{6,5},{7,6},{8,7},{9,8},{10,9},{11,1... | collective-permute-start | bytes 393224 | tf_op jit(solution)/shard_map/ppermute | solution.py:19
Sparse Core Ops, SparseCore 0:
  151.6 224.6 all-reduce.2
where the time goes:
time: 388 us; the launch traced here: 387 us
  local copies, waits for them, and re-layouts  219 us (56%)
  waiting for transfers between devices  107 us (28%)
  starting transfers between devices  21.2 us (5%)
  matrix products  16.8 us (4%)
  between operations  14.3 us (4%)
  other arithmetic  8.39 us (2%)
    gather x2, local copies, waits for them, and re-layouts, per_device(): grad_gathered = grad_lookup[local_ids.T].reshape(row_count, 27 * feat_width)  109 us
    psum x1, waiting for transfers between devices, per_device(): conv_total, down_total = lax.psum((conv_local, down_local), 'space')  105 us
    gather x1, local copies, waits for them, and re-layouts, per_device(): gathered = lookup[local_ids.T].reshape(row_count, 27 * feat_width)  96.4 us
    reshape x1, local copies, waits for them, and re-layouts, per_device(): gathered = lookup[local_ids.T].reshape(row_count, 27 * feat_width)  10.1 us
    ppermute x2, starting transfers between devices, shifted(): return lax.ppermute(value, axis, pairs)  8.59 us
    dot_general x1, matrix products, per_device(): jnp.dot(grad_gathered, flipped, preferred_element_type=jnp.float32)  8.26 us
  transfers between devices with their start and end apart: 7, of which 3 were waited for; matrix products, arithmetic and copies ran while one was open for 32% of the time, Pallas kernels for 0%

commit v1 on v0

v1 whole, which is shorter than its diff:
```python
import functools
import math

import jax
import jax.numpy as jnp
from jax import lax
from jax.experimental import pallas as pl
from jax.experimental.pallas import tpu as pltpu
from jax.sharding import PartitionSpec as P

F32 = jnp.float32
BF16 = jnp.bfloat16
C = 64
C2 = 128
V = 1024
HALF = 512
VC = 256
SY, SZ = 32, 16
LAYER = SY * SZ
CELLS = 4 * LAYER
WIDE = CELLS + 2 * LAYER
EMPTY = 3 * V
TAPS = 9 * C
ROWS_A, ROWS_B = 768, 640
CHIPS = {128: (4, 8, 4), 16: (2, 2, 4)}


def dot(a, b):
    return jnp.dot(a, b, preferred_element_type=F32)


def dot_nt(a, b):
    return lax.dot_general(a, b, (((1,), (1,)), ((), ())), preferred_element_type=F32)


def dot_tn(a, b):
    return lax.dot_general(a, b, (((0,), (0,)), ((), ())), preferred_element_type=F32)


def hot(rows, ids, start):
    at = lax.broadcasted_iota(jnp.int32, (rows, ids.shape[1]), 0) + start
    return jnp.where(at == ids, 1.0, 0.0).astype(BF16)


def peer(place, dims, axis, step):
    _, nz, ny = dims
    y, z, x = place % ny, place // ny % nz, place // (ny * nz)
    if axis == "y":
        return place - y + (y + step) % ny
    if axis == "z":
        return place + ((z + step) % nz - z) * ny
    return place + ((x + step) % dims[0] - x) * (ny * nz)


def greet(partners):
    barrier = pltpu.get_barrier_semaphore()
    for other in partners:
        pl.semaphore_signal(
            barrier, inc=1, device_id={"space": other}, device_id_type=pl.DeviceIdType.MESH
        )
    pl.semaphore_wait(barrier, len(partners))


def push(src, dst, send, recv, other):
    copy = pltpu.make_async_remote_copy(
        src_ref=src,
        dst_ref=dst,
        send_sem=send,
        recv_sem=recv,
        device_id={"space": other},
        device_id_type=pl.DeviceIdType.MESH,
    )
    copy.start()
    return copy


def halo_kernel(
    count, feats, table, grads, prev_f, next_f, prev_t, next_t, prev_g, send, recv
):
    place = lax.axis_index("space")
    after, before = (place + 1) % count, (place + count - 1) % count
    greet((after, before))
    copies = [
        push(feats.at[:, pl.ds(HALF, HALF)], prev_f, send.at[0], recv.at[0], after),
        push(feats.at[:, pl.ds(0, HALF)], next_f, send.at[1], recv.at[1], before),
        push(table.at[:, pl.ds(HALF, HALF)], prev_t, send.at[2], recv.at[2], after),
        push(table.at[:, pl.ds(0, HALF)], next_t, send.at[3], recv.at[3], before),
        push(grads, prev_g, send.at[4], recv.at[4], after),
    ]
    for copy in copies:
        copy.wait()


def cell_maps(table, prev_t, next_t, own_hot, prev_hot, next_hot):
    own = table[0:1, :].astype(jnp.int32)
    has_prev, has_next = table[3:4, 0:HALF], table[4:5, 0:HALF]
    prev = jnp.where(has_prev > 0.0, prev_t[0:1, :], -1.0).astype(jnp.int32)
    after = jnp.where(has_next > 0.0, next_t[0:1, :], -1.0).astype(jnp.int32)
    for start in range(0, CELLS, 256):
        own_hot[start : start + 256, :] = hot(256, own, start)
    prev_hot[...] = hot(LAYER, prev, 3 * LAYER)
    next_hot[...] = hot(LAYER, after, 0)


def edge_masks():
    lane = lax.broadcasted_iota(jnp.int32, (1, WIDE), 1)
    y, z = lane // SZ % SY, lane % SZ
    masks = []
    for dy in (-1, 0, 1):
        for dz in (-1, 0, 1):
            inside = (y + dy >= 0) & (y + dy < SY) & (z + dz >= 0) & (z + dz < SZ)
            masks.append(jnp.where(inside, 1.0, 0.0))
    return masks


def shifted(block, tap, masks):
    step = (tap // 3 - 1) * SZ + tap % 3 - 1
    if step == 0:
        return block
    return pltpu.roll(block, (-step) % WIDE, 1) * masks[tap]


def unfold(wide, masks, taps):
    for group in range(0, C, 16):
        block = wide[group : group + 16, :]
        for tap in range(9):
            taps[tap * C + group : tap * C + group + 16, :] = shifted(block, tap, masks).astype(
                BF16
            )


def fold(spread):
    return (
        spread[0:C, 0:CELLS]
        + spread[C : 2 * C, LAYER : LAYER + CELLS]
        + spread[2 * C : 3 * C, 2 * LAYER : 2 * LAYER + CELLS]
    )


def to_voxels(cells, own_hot):
    high = cells.astype(BF16)
    low = (cells - high.astype(F32)).astype(BF16)
    both = dot(jnp.concatenate([high, low], axis=0), own_hot[...])
    return both[0:C] + both[C : 2 * C]


def named_rows(names, rows, candidates):
    for start in range(0, CELLS, 256):
        rows[start : start + 256, :] = hot(256, names, start + HALF)
    return dot(candidates, rows[...]).astype(BF16)


def pieces(ids):
    high = lax.shift_right_logical(ids, 6)
    return high.astype(F32), (ids & 63).astype(F32)


def block_kernel(
    feats, prev_f, next_f, table, prev_t, next_t, nbr, w_conv, w_down, grads, prev_g,
    grad_pre, back, part_a, part_b, coarse_own, coarse_prev, flag,
    own_hot, prev_hot, next_hot, wide, taps, stack, named, preact, conv, lookup, parent_hot, spread,
):
    cell_maps(table, prev_t, next_t, own_hot, prev_hot, next_hot)
    masks = edge_masks()

    lane = lax.broadcasted_iota(jnp.int32, (1, V), 1)
    named[...] = jnp.zeros_like(named)
    named[0:27, :] = EMPTY - nbr[...]
    named[27:28, :] = 2 * V - lane
    high, low = pieces(named[...])
    own = jnp.concatenate([feats[...], high.astype(BF16), low.astype(BF16)], axis=0)
    own = dot_nt(own, own_hot[...])
    wide[0:C, LAYER : LAYER + CELLS] = own[0:C]
    told = own[C : C + 32] * 64.0 + own[C + 32 : C + 64]
    row = lax.broadcasted_iota(jnp.int32, (16, HALF), 0)
    half_lane = lax.broadcasted_iota(jnp.int32, (16, HALF), 1)
    for edge, where_hot, ids, at in (
        (prev_f, prev_hot, EMPTY - HALF - half_lane, 0),
        (next_f, next_hot, V - half_lane, LAYER + CELLS),
    ):
        high, low = pieces(ids)
        tail = jnp.where(row == 0, high, jnp.where(row == 1, low, 0.0)).astype(BF16)
        placed = dot_nt(jnp.concatenate([edge[...], tail], axis=0), where_hot[...])
        wide[0:C, at : at + LAYER] = placed[0:C]
        wide[C : C + 8, at : at + LAYER] = jnp.broadcast_to(
            placed[C : C + 1] * 64.0 + placed[C + 1 : C + 2], (8, LAYER)
        )
    wide[C : C + 8, LAYER : LAYER + CELLS] = jnp.broadcast_to(told[27:28], (8, CELLS))

    ids = wide[C : C + 8, :]
    wrong = jnp.zeros((1, CELLS), F32)
    for tap in range(9):
        seen = shifted(ids, tap, masks)[0:1]
        for layer in range(3):
            k = layer * 9 + tap
            wrong = jnp.maximum(
                wrong, jnp.abs(told[k : k + 1] - seen[:, layer * LAYER : layer * LAYER + CELLS])
            )
    wrong = jnp.max(jnp.where(told[27:28] > 0.0, wrong, 0.0))
    outside = jnp.min(table[0:1, :])
    general = jnp.logical_or(wrong > 0.0, outside < 0.0)
    flag[0] = jnp.where(general, 1, 0)

    unfold(wide, masks, taps)
    weights = jnp.concatenate(
        [w_conv[:, d * TAPS : (d + 1) * TAPS] for d in range(3)], axis=0
    )
    preact[...] = to_voxels(fold(dot(weights, taps[...])), own_hot)

    candidates = lambda: jnp.concatenate([prev_f[...], feats[...], next_f[...]], axis=1)

    @pl.when(general)
    def _():
        preact[...] = jnp.zeros_like(preact)
        rows = candidates()

        def pair(i, carry):
            block = w_conv[:, pl.ds(pl.multiple_of(i * 128, 128), 128)]
            for half in range(2):
                read = named_rows(nbr[pl.ds(2 * i + half, 1), :], own_hot, rows)
                preact[...] += dot(block[:, half * C : (half + 1) * C], read)
            return carry

        lax.fori_loop(0, 13, pair, 0)
        preact[...] += dot(w_conv[:, 26 * C : 27 * C], named_rows(nbr[26:27, :], own_hot, rows))

    act = preact[...]
    gate = jax.nn.sigmoid(act)
    middle = (feats[...].astype(F32) + act * gate).astype(BF16)

    lookup[0:VC, :] = prev_g[...]
    lookup[VC : 2 * VC, :] = grads[...]
    parent_hot[...] = hot(2 * VC, table[1:2, :].astype(jnp.int32), 0)
    parent_grads = dot_tn(lookup[...], parent_hot[...]).astype(BF16)
    back_all = dot(w_down[...], parent_grads)
    octant = table[2:3, :]
    total = jnp.zeros((C, V), F32)
    for o in range(8):
        chosen = jnp.broadcast_to(octant == float(o), (C, V))
        total += jnp.where(chosen, back_all[o * C : (o + 1) * C], 0.0)
        spread[o * C : (o + 1) * C, :] = jnp.where(chosen, middle.astype(F32), 0.0).astype(BF16)
    back[...] = total
    children = dot_nt(spread[...], parent_hot[...]).astype(BF16)
    sums = dot_tn(children, w_down[...])
    coarse_prev[...] = sums[0:VC].astype(BF16)
    coarse_own[...] = sums[VC : 2 * VC]
    part_b[128:ROWS_B, :] = dot(children, lookup[...])

    slope = (total * gate * (1.0 + act * (1.0 - gate))).astype(BF16)
    grad_pre[...] = slope

    @pl.when(jnp.logical_not(general))
    def _():
        placed = dot_nt(slope, own_hot[...]).astype(BF16)
        stack[...] = jnp.zeros_like(stack)
        for d in range(3):
            stack[d * C : (d + 1) * C, d * LAYER : d * LAYER + CELLS] = placed
        product = dot_nt(stack[...], taps[...])
        flat = jnp.concatenate([product[d * C : (d + 1) * C] for d in range(3)], axis=1)
        conv[:, 27 * C : 28 * C] = jnp.zeros((C, C), F32)
        conv[:, 0 : 27 * C] = flat

    @pl.when(general)
    def _():
        rows = candidates()
        slopes = grad_pre[...]

        def pair(i, carry):
            both = [
                dot_nt(slopes, named_rows(nbr[pl.ds(2 * i + half, 1), :], own_hot, rows))
                for half in range(2)
            ]
            conv[:, pl.ds(pl.multiple_of(i * 128, 128), 128)] = jnp.concatenate(both, axis=1)
            return carry

        lax.fori_loop(0, 13, pair, 0)
        last = dot_nt(slopes, named_rows(nbr[26:27, :], own_hot, rows))
        conv[:, 26 * C : 28 * C] = jnp.concatenate([last, jnp.zeros_like(last)], axis=1)

    for t in range(12):
        part_a[t * C : (t + 1) * C, :] = conv[:, t * 128 : (t + 1) * 128]
    for t in range(2):
        part_b[t * C : (t + 1) * C, :] = conv[:, (12 + t) * 128 : (13 + t) * 128]


def total_kernel(
    count, dims, grad_pre, coarse, part_a, part_b,
    prev_p, next_p, coarse_in, done,
    got_a1, got_b1, sum_a1, sum_b1, got_a2, got_b2, got_z,
    halo_send, halo_recv, send_a, recv_a, send_b, recv_b, send_z, recv_z, send_g, recv_g,
):
    nx, nz, ny = dims
    place = lax.axis_index("space")
    y, z, x = place % ny, place // ny % nz, place // (ny * nz)
    after, before = (place + 1) % count, (place + count - 1) % count
    ys = [peer(place, dims, "y", d) for d in range(1, ny)]
    xs = [peer(place, dims, "x", d) for d in range(1, nx)]
    zs = [peer(place, dims, "z", d) for d in range(1, nz)]
    greet([after, before] + ys + xs + zs)

    first = []
    for d in range(1, ny):
        first.append(
            push(part_a.at[(y + d) % ny], got_a1.at[d - 1], send_a.at[0, d - 1], recv_a.at[0, d - 1], ys[d - 1])
        )
    for d in range(1, nx):
        first.append(
            push(part_b.at[(x + d) % nx], got_b1.at[d - 1], send_b.at[0, d - 1], recv_b.at[0, d - 1], xs[d - 1])
        )
    halos = [
        push(grad_pre.at[:, pl.ds(HALF, HALF)], prev_p, halo_send.at[0], halo_recv.at[0], after),
        push(grad_pre.at[:, pl.ds(0, HALF)], next_p, halo_send.at[1], halo_recv.at[1], before),
        push(coarse, coarse_in, halo_send.at[2], halo_recv.at[2], before),
    ]
    for copy in first:
        copy.wait()
    size_a, size_b = ROWS_A // (ny * nx), ROWS_B // (ny * nx)
    total = part_a[y]
    for d in range(ny - 1):
        total += got_a1[d]
    for i in range(nx):
        sum_a1[i] = total[i * size_a : (i + 1) * size_a]
    total = part_b[x]
    for d in range(nx - 1):
        total += got_b1[d]
    for i in range(ny):
        sum_b1[i] = total[i * size_b : (i + 1) * size_b]
    second = []
    for d in range(1, nx):
        second.append(
            push(sum_a1.at[(x + d) % nx], got_a2.at[d - 1], send_a.at[1, d - 1], recv_a.at[1, d - 1], xs[d - 1])
        )
    for d in range(1, ny):
        second.append(
            push(sum_b1.at[(y + d) % ny], got_b2.at[d - 1], send_b.at[1, d - 1], recv_b.at[1, d - 1], ys[d - 1])
        )
    for copy in second:
        copy.wait()
    total = sum_a1[x]
    for d in range(nx - 1):
        total += got_a2[d]
    got_z[z, 0:size_a, :] = total
    total = sum_b1[y]
    for d in range(ny - 1):
        total += got_b2[d]
    got_z[z, size_a : size_a + size_b, :] = total

    third = [
        push(got_z.at[z], got_z.at[z], send_z.at[d - 1], recv_z.at[d - 1], zs[d - 1])
        for d in range(1, nz)
    ]
    for copy in third:
        copy.wait()
    total = got_z[0]
    for i in range(1, nz):
        total += got_z[i]
    done[x, y, 0, 0:size_a, :] = total[0:size_a].astype(BF16)
    done[x, y, 1, 0:size_b, :] = total[size_a : size_a + size_b].astype(BF16)

    fourth = [
        push(done.at[x, y, 0], done.at[x, y, 0], send_g.at[0, d - 1], recv_g.at[0, d - 1], xs[d - 1])
        for d in range(1, nx)
    ] + [
        push(done.at[x, y, 1], done.at[x, y, 1], send_g.at[1, d - 1], recv_g.at[1, d - 1], ys[d - 1])
        for d in range(1, ny)
    ]
    for copy in fourth:
        copy.wait()
    fifth = [
        push(done.at[:, y, 0], done.at[:, y, 0], send_g.at[2, d - 1], recv_g.at[2, d - 1], ys[d - 1])
        for d in range(1, ny)
    ] + [
        push(done.at[x, :, 1], done.at[x, :, 1], send_g.at[3, d - 1], recv_g.at[3, d - 1], xs[d - 1])
        for d in range(1, nx)
    ]
    for copy in fifth + halos:
        copy.wait()


def finish_kernel(
    dims, scale, flag, grad_pre, prev_p, next_p, table, prev_t, next_t, nbr, w_conv, back, coarse_own,
    coarse_in, done, coarse_out, grad_feats, grad_conv, grad_down,
    own_hot, prev_hot, next_hot, wide, taps, weights, spill, flat,
):
    nx, _, ny = dims
    cell_maps(table, prev_t, next_t, own_hot, prev_hot, next_hot)
    masks = edge_masks()
    wide[:, 0:LAYER] = dot_nt(prev_p[...], prev_hot[...])
    wide[:, LAYER : LAYER + CELLS] = dot_nt(grad_pre[...], own_hot[...])
    wide[:, LAYER + CELLS : WIDE] = dot_nt(next_p[...], next_hot[...])
    unfold(wide, masks, taps)
    for layer in range(3):
        for tap in range(9):
            k = 26 - (layer * 9 + tap)
            weights[tap * C : (tap + 1) * C, layer * C : (layer + 1) * C] = w_conv[
                :, k * C : (k + 1) * C
            ]
    spill[...] = to_voxels(fold(dot_tn(weights[...], taps[...])), own_hot)

    @pl.when(flag[0] > 0)
    def _():
        rows = jnp.concatenate([prev_p[...], grad_pre[...], next_p[...]], axis=1)
        spill[...] = dot_tn(
            w_conv[:, 26 * C : 27 * C], named_rows(nbr[0:1, :], own_hot, rows)
        )

        def pair(i, carry):
            block = w_conv[:, pl.ds(pl.multiple_of(i * 128, 128), 128)]
            for half in range(2):
                read = named_rows(nbr[pl.ds(26 - 2 * i - half, 1), :], own_hot, rows)
                spill[...] += dot_tn(block[:, half * C : (half + 1) * C], read)
            return carry

        lax.fori_loop(0, 13, pair, 0)

    grad_feats[...] = (back[...] + spill[...]).astype(BF16)
    coarse_out[...] = (coarse_own[...] + coarse_in[...].astype(F32)).astype(BF16)
    size_a, size_b = ROWS_A // (ny * nx), ROWS_B // (ny * nx)
    for i in range(nx):
        for j in range(ny):
            at = (j * nx + i) * size_a
            flat[at : at + size_a, :] = done[i, j, 0, 0:size_a, :].astype(F32) * scale
            at = ROWS_A + (i * ny + j) * size_b
            flat[at : at + size_b, :] = done[i, j, 1, 0:size_b, :].astype(F32) * scale
    for t in range(13):
        grad_conv[:, t * 128 : (t + 1) * 128] = flat[t * C : (t + 1) * C, :]
    grad_conv[:, 13 * 128 : 27 * C] = flat[13 * C : 14 * C, 0:C]
    grad_down[...] = flat[14 * C : 14 * C + 8 * C, :]


def vmem(n):
    return [pl.BlockSpec(memory_space=pltpu.VMEM)] * n


def shape(dims, dtype):
    return jax.ShapeDtypeStruct(dims, dtype)


def per_device(feats, w_conv, w_down, neighbors, parent, octant, grad_out):
    count = lax.axis_size("space")
    dims = CHIPS[count]
    nx, nz, ny = dims
    place = lax.axis_index("space")
    feats, w_conv = feats.T, w_conv.T

    own_start = place * VC
    prev_start = (place - 1) % count * VC
    inside = (parent >= own_start) & (parent < own_start + VC)
    coarse = jnp.where(inside, parent - own_start + VC, parent - prev_start)
    layer = coarse // 128 - 1
    cell = (
        (2 * layer + octant // 4) * LAYER
        + (2 * (coarse % 128 // 8) + octant // 2 % 2) * SZ
        + 2 * (coarse % 8)
        + octant % 2
    )
    cell = jnp.where((layer == 0) | (layer == 1), cell, -1)
    ones = jnp.ones_like(cell)
    zeros = jnp.zeros_like(cell)
    table = jnp.stack(
        [
            cell, coarse, octant,
            jnp.where(place > 0, ones, zeros), jnp.where(place < count - 1, ones, zeros),
            zeros, zeros, zeros,
        ]
    ).astype(F32)

    dma = pltpu.SemaphoreType.DMA
    prev_f, next_f, prev_t, next_t, prev_g = pl.pallas_call(
        functools.partial(halo_kernel, count),
        name="halo",
        out_shape=(
            shape((C, HALF), BF16), shape((C, HALF), BF16),
            shape((8, HALF), F32), shape((8, HALF), F32), shape((VC, C2), BF16),
        ),
        in_specs=vmem(3),
        out_specs=tuple(vmem(5)),
        scratch_shapes=[dma((5,)), dma((5,))],
        compiler_params=pltpu.CompilerParams(collective_id=0, has_side_effects=True),
    )(feats, table, grad_out)

    maps = [
        pltpu.VMEM((CELLS, V), BF16), pltpu.VMEM((LAYER, HALF), BF16), pltpu.VMEM((LAYER, HALF), BF16),
    ]
    grad_pre, back, part_a, part_b, coarse_own, coarse_prev, flag = pl.pallas_call(
        block_kernel,
        name="block",
        out_shape=(
            shape((C, V), BF16), shape((C, V), F32), shape((ROWS_A, C2), F32), shape((ROWS_B, C2), F32),
            shape((VC, C2), F32), shape((VC, C2), BF16), shape((1,), jnp.int32),
        ),
        in_specs=vmem(11),
        out_specs=tuple(vmem(6) + [pl.BlockSpec(memory_space=pltpu.SMEM)]),
        scratch_shapes=maps
        + [
            pltpu.VMEM((C + 8, WIDE), F32), pltpu.VMEM((TAPS, WIDE), BF16), pltpu.VMEM((3 * C, WIDE), BF16),
            pltpu.VMEM((32, V), jnp.int32), pltpu.VMEM((C, V), F32), pltpu.VMEM((C, 28 * C), F32),
            pltpu.VMEM((2 * VC, C2), BF16), pltpu.VMEM((2 * VC, V), BF16), pltpu.VMEM((8 * C, V), BF16),
        ],
    )(feats, prev_f, next_f, table, prev_t, next_t, neighbors, w_conv, w_down, grad_out, prev_g)

    size_a, size_b = ROWS_A // (nx * ny), ROWS_B // (nx * ny)
    most = max(nx, ny) - 1
    prev_p, next_p, coarse_in, done = pl.pallas_call(
        functools.partial(total_kernel, count, dims),
        name="total",
        out_shape=(
            shape((C, HALF), BF16), shape((C, HALF), BF16), shape((VC, C2), BF16),
            shape((nx, ny, 2, size_a, C2), BF16),
        ),
        in_specs=vmem(4),
        out_specs=tuple(vmem(4)),
        scratch_shapes=[
            pltpu.VMEM((ny - 1, ROWS_A // ny, C2), F32), pltpu.VMEM((nx - 1, ROWS_B // nx, C2), F32),
            pltpu.VMEM((nx, size_a, C2), F32), pltpu.VMEM((ny, size_b, C2), F32),
            pltpu.VMEM((nx - 1, size_a, C2), F32), pltpu.VMEM((ny - 1, size_b, C2), F32),
            pltpu.VMEM((nz, size_a + size_b, C2), F32),
            dma((3,)), dma((3,)), dma((2, most)), dma((2, most)), dma((2, most)), dma((2, most)),
            dma((nz - 1,)), dma((nz - 1,)), dma((4, most)), dma((4, most)),
        ],
        compiler_params=pltpu.CompilerParams(collective_id=1, has_side_effects=True),
    )(
        grad_pre, coarse_prev,
        part_a.reshape(ny, ROWS_A // ny, C2), part_b.reshape(nx, ROWS_B // nx, C2),
    )

    coarse_out, grad_feats, grad_conv, grad_down = pl.pallas_call(
        functools.partial(finish_kernel, dims, 1.0 / math.sqrt(V * count)),
        name="finish",
        out_shape=(
            shape((VC, C2), BF16), shape((C, V), BF16), shape((C, 27 * C), F32), shape((8 * C, C2), F32),
        ),
        in_specs=[pl.BlockSpec(memory_space=pltpu.SMEM)] + vmem(12),
        out_specs=tuple(vmem(4)),
        scratch_shapes=maps
        + [
            pltpu.VMEM((C, WIDE), F32), pltpu.VMEM((TAPS, WIDE), BF16), pltpu.VMEM((TAPS, 3 * C), BF16),
            pltpu.VMEM((C, V), F32), pltpu.VMEM((ROWS_A + ROWS_B, C2), F32),
        ],
    )(
        flag, grad_pre, prev_p, next_p, table, prev_t, next_t, neighbors, w_conv, back, coarse_own,
        coarse_in, done,
    )
    return coarse_out, grad_feats.T, grad_conv.T, grad_down


def solution(mesh):
    rows = P(("dp", "space"), None)
    line = P(("dp", "space"))
    return jax.shard_map(
        per_device,
        mesh=mesh,
        in_specs=(rows, P(), P(), P(None, ("dp", "space")), line, line, rows),
        out_specs=(rows, rows, P("dp", None), P("dp", None)),
        check_vma=False,
    )
```

time: 388 us -> 72.4 us (0.19)
  local copies, waits for them, and re-layouts: 219 us -> 0.74 us
  waiting for transfers between devices: 107 us -> 0 us
  Pallas kernels: 0 us -> 70.1 us
  starting transfers between devices: 21.2 us -> 0 us
  matrix products: 16.8 us -> 0 us
  between operations: 14.3 us -> 0.74 us
  other arithmetic: 8.39 us -> 0.64 us
    gather x3 -> x0, local copies, waits for them, and re-layouts: 205 us -> none  [the longest x2 109 us: per_device(): grad_gathered = grad_lookup[local_ids.T].reshape(row_count, 27 * feat_width)]
    psum x1 -> x0, waiting for transfers between devices: 105 us -> none  [per_device(): conv_total, down_total = lax.psum((conv_local, down_local), 'space')]
    pallas_call x0 -> x4, Pallas kernels: none -> 70.1 us  [the longest x1 36 us: per_device(): pl.pallas_call(functools.partial(total_kernel, count, dims), name='total'...]
    ppermute x6 -> x0, starting transfers between devices: 21.1 us -> none  [the longest x2 8.59 us: shifted(): return lax.ppermute(value, axis, pairs)]
    dot_general x7 -> x0, matrix products: 16.8 us -> none  [the longest x1 8.26 us: per_device(): jnp.dot(grad_gathered, flipped, preferred_element_type=jnp.float32)]
    reshape x2 -> x0, local copies, waits for them, and re-layouts: 11.5 us -> none  [the longest x1 10.1 us: per_device(): gathered = lookup[local_ids.T].reshape(row_count, 27 * feat_width)]
  transfers between devices with their start and end apart: 7 -> 0, of which waited for: 3 -> 0; matrix products, arithmetic and copies ran while one was open for 32% -> 0% of each run, Pallas kernels for 0% -> 0%
where the time goes in v1:
time: 72.4 us; the launch traced here: 72.2 us
  Pallas kernels  70.1 us (97%)
  local copies, waits for them, and re-layouts  0.74 us (1%)
  between operations  0.74 us (1%)
    pallas_call x1, Pallas kernels, per_device(): pl.pallas_call(functools.partial(total_kernel, count, dims), name='total'...  36 us
    pallas_call x1, Pallas kernels, per_device(): pl.pallas_call(functools.partial(halo_kernel, count), name='halo', out_sh...  16.2 us
    pallas_call x1, Pallas kernels, per_device(): pl.pallas_call(block_kernel, name='block', out_shape=(shape((C, V), BF16)...  11.2 us
    pallas_call x1, Pallas kernels, per_device(): pl.pallas_call(functools.partial(finish_kernel, dims, 1.0 / math.sqrt(V *...  6.68 us

profile of v1, /device:TPU:8, one launch (start us, length us, event | category | flops | bytes accessed | tf_op | source)
XLA Modules:
  0.0 72.2 jit_solution(9066707801680193732)
XLA Ops:
  0.7 0.0 copy-start
  0.7 0.0 copy-start.1
  0.7 0.6 copy-done
  1.4 0.0 copy-done.1
  1.4 0.1 stack.27
  1.5 0.6 convert_element_type.3.table
  2.1 16.2 %halo.1 = (bf16[64,512]{1,0:T(8,128)(2,1)}, bf16[64,512]{1,0:T(8,128)(2,1)}, f32[8,512]{1,0:T(8,128)}, f32[8,512]{1,0:T(8,128)}, bf16[256,128]{1,0:T(8,128)(2,1)}) custom-call(bf16[64,1024]{1,0:T(8,128)(2,1)} %bitcast.11, f32[8,1024]{1,0:T(8,128)} %convert_element_type.3.table, bf16[256,128]{1,0:T(8,128)(2,1)} %grads.3), custom_call_target="tpu_custom_call" | custom-call | tf_op jit(solution)/shard_map/halo/pallas_call | solution.py:469
  18.3 11.2 %block.1 = (bf16[64,1024]{1,0:T(8,128)(2,1)}, f32[64,1024]{1,0:T(8,128)}, f32[768,128]{1,0:T(8,128)}, f32[640,128]{1,0:T(8,128)}, f32[256,128]{1,0:T(8,128)}, /*index=5*/bf16[256,128]{1,0:T(8,128)(2,1)}, s32[1]{0:T(128)}) custom-call(bf16[64,1024]{1,0:T(8,128)(2,1)} %bitcast.12, bf16[64,512]{1,0:T(8,128)(2,1)} %get-tuple-element.24.prev_f, ...), custom_call_target="tpu_custom_call" | custom-call | tf_op jit(solution)/shard_map/block/pallas_call | solution.py:485
  29.6 36.0 %total.1 = (bf16[64,512]{1,0:T(8,128)(2,1)}, bf16[64,512]{1,0:T(8,128)(2,1)}, bf16[256,128]{1,0:T(8,128)(2,1)}, bf16[4,4,2,48,128]{4,3,2,1,0:T(8,128)(2,1)}) custom-call(bf16[64,1024]{1,0:T(8,128)(2,1)} %get-tuple-element.30.grad_pre, bf16[256,128]{1,0:T(8,128)(2,1)} %get-tuple-element.31.coarse, f32[4,192,128]{2,1,0:T(8,128)} %bitcast.13, ...), custom_call_target="tpu_custom_call" | custom-call | tf_op jit(solution)/shard_map/total/pallas_call | solution.py:504
  65.5 6.7 %finish.1 = (bf16[256,128]{1,0:T(8,128)(2,1)}, bf16[64,1024]{1,0:T(8,128)(2,1)}, f32[64,1728]{1,0:T(8,128)}, f32[512,128]{1,0:T(8,128)}) custom-call(s32[1]{0:T(128)} %get-tuple-element.29.flag, bf16[64,1024]{1,0:T(8,128)(2,1)} %get-tuple-element.30.grad_pre, bf16[64,512]{1,0:T(8,128)(2,1)} %get-tuple-element.34.prev_p, ...), custom_call_target="tpu_custom_call" | custom-call | tf_op jit(solution)/shard_map/finish/pallas_call | solution.py:527
  (5 shorter events, 0.0 us)
Async XLA Ops:
  0.7 0.7 copy-start
  0.7 0.7 copy-start.1

commit v2 on v1

v2 whole, which is shorter than its diff:
```python
import functools
import math

import jax
import jax.numpy as jnp
from jax import lax
from jax.experimental import pallas as pl
from jax.experimental.pallas import tpu as pltpu
from jax.sharding import PartitionSpec as P

F32 = jnp.float32
BF16 = jnp.bfloat16
C = 64
C2 = 128
V = 1024
HALF = 512
VC = 256
SY, SZ = 32, 16
LAYER = SY * SZ
CELLS = 4 * LAYER
WIDE = CELLS + 2 * LAYER
EMPTY = 3 * V
TAPS = 9 * C
ROWS_A, ROWS_B = 768, 640
CHIPS = {128: (4, 8, 4), 16: (2, 2, 4)}


def dot(a, b):
    return jnp.dot(a, b, preferred_element_type=F32)


def dot_nt(a, b):
    return lax.dot_general(a, b, (((1,), (1,)), ((), ())), preferred_element_type=F32)


def dot_tn(a, b):
    return lax.dot_general(a, b, (((0,), (0,)), ((), ())), preferred_element_type=F32)


def fill_hot(ref, ids, first):
    high = jnp.broadcast_to(
        lax.shift_right_arithmetic(ids, 4).astype(F32).astype(BF16), (16, ids.shape[1])
    )
    row = lax.broadcasted_iota(jnp.int32, high.shape, 0)
    low = jnp.where(row == (ids & 15), 1.0, 0.0).astype(BF16)
    none = jnp.zeros_like(low)
    for t in range(ref.shape[0] // 16):
        ref[t * 16 : (t + 1) * 16, :] = jnp.where(
            high == jnp.asarray(first // 16 + t, BF16), low, none
        )


def peer(place, dims, axis, step):
    _, nz, ny = dims
    y, z, x = place % ny, place // ny % nz, place // (ny * nz)
    if axis == "y":
        return place - y + (y + step) % ny
    if axis == "z":
        return place + ((z + step) % nz - z) * ny
    return place + ((x + step) % dims[0] - x) * (ny * nz)


def greet(partners):
    barrier = pltpu.get_barrier_semaphore()
    for other in partners:
        pl.semaphore_signal(
            barrier, inc=1, device_id={"space": other}, device_id_type=pl.DeviceIdType.MESH
        )
    pl.semaphore_wait(barrier, len(partners))


def push(src, dst, send, recv, other):
    copy = pltpu.make_async_remote_copy(
        src_ref=src,
        dst_ref=dst,
        send_sem=send,
        recv_sem=recv,
        device_id={"space": other},
        device_id_type=pl.DeviceIdType.MESH,
    )
    copy.start()
    return copy


def places(count, place, parent, octant):
    own, prev = place * VC, (place + count - 1) % count * VC
    inside = (parent >= own) & (parent < own + VC)
    coarse = jnp.where(inside, parent - own + VC, parent - prev)
    layer = lax.shift_right_arithmetic(coarse, 7) - 1
    cell = (
        (2 * layer + lax.shift_right_arithmetic(octant, 2)) * LAYER
        + (2 * lax.shift_right_arithmetic(coarse & 127, 3) + (lax.shift_right_arithmetic(octant, 1) & 1)) * SZ
        + 2 * (coarse & 7)
        + (octant & 1)
    )
    return coarse, jnp.where((layer == 0) | (layer == 1), cell, -1)


def edge_masks():
    lane = lax.broadcasted_iota(jnp.int32, (1, LAYER), 1)
    y, z = lax.shift_right_arithmetic(lane, 4), lane & (SZ - 1)
    masks = []
    for dy in (-1, 0, 1):
        for dz in (-1, 0, 1):
            inside = (y + dy >= 0) & (y + dy < SY) & (z + dz >= 0) & (z + dz < SZ)
            masks.append(jnp.where(inside, 1.0, 0.0))
    return masks


def shifted(block, tap, masks):
    step = (tap // 3 - 1) * SZ + tap % 3 - 1
    if step == 0:
        return block
    rows = block.shape[0]
    mask = jnp.broadcast_to(masks[tap], (rows, LAYER)).astype(block.dtype)
    return pltpu.roll(block, (-step) % WIDE, 1) * jnp.concatenate([mask] * (WIDE // LAYER), axis=1)


def unfold(wide, masks, taps):
    for group in range(0, C, 16):
        block = wide[group : group + 16, :]
        for tap in range(9):
            taps[tap * C + group : tap * C + group + 16, :] = shifted(block, tap, masks)


def split(x):
    high = x.astype(BF16)
    return high, (x - high.astype(F32)).astype(BF16)


def named_rows(names, rows, candidates):
    fill_hot(rows, names, HALF)
    return dot(candidates, rows[...]).astype(BF16)


def pieces(ids):
    return lax.shift_right_logical(ids, 6).astype(F32), (ids & 63).astype(F32)


def octant_order(flip):
    shape_ = (256, 256)
    cell = lax.broadcasted_iota(jnp.int32, shape_, 1 if flip else 0)
    slot = lax.broadcasted_iota(jnp.int32, shape_, 0 if flip else 1)
    corner, pair = lax.shift_right_arithmetic(slot, 6), slot & 63
    y = 2 * lax.shift_right_arithmetic(pair, 3) + lax.shift_right_arithmetic(corner, 1)
    z = 2 * (pair & 7) + (corner & 1)
    return jnp.where(cell == y * SZ + z, 1.0, 0.0).astype(BF16)


def store_conv(conv, part_a, part_b):
    for t in range(12):
        part_a[t * C : (t + 1) * C, :] = conv[:, t * 128 : (t + 1) * 128]
    for t in range(2):
        part_b[t * C : (t + 1) * C, :] = conv[:, (12 + t) * 128 : (13 + t) * 128]


def block_kernel(
    count, feats, parent, octant, nbr, w_conv, w_down, grads,
    grad_pre, slopes, back, part_a, part_b, coarse_own, coarse_prev, wrong, table, edges,
    prev_f, next_f, prev_g,
    prev_p, next_p, prev_o, next_o, own_hot, prev_hot, next_hot, wide, ids, seen, taps, stack, named,
    conv, spread, lookup, send, recv,
):
    place = lax.axis_index("space")
    after, before = (place + 1) % count, (place + count - 1) % count
    greet((after, before))
    late, early = pl.ds(HALF, HALF), pl.ds(0, HALF)
    marks = [
        push(parent.at[:, late], prev_p, send.at[0], recv.at[0], after),
        push(octant.at[:, late], prev_o, send.at[1], recv.at[1], after),
        push(parent.at[:, early], next_p, send.at[2], recv.at[2], before),
        push(octant.at[:, early], next_o, send.at[3], recv.at[3], before),
    ]
    halos = [
        push(feats.at[:, late], prev_f, send.at[4], recv.at[4], after),
        push(feats.at[:, early], next_f, send.at[5], recv.at[5], before),
    ]
    coarse_halo = push(grads, prev_g, send.at[6], recv.at[6], after)

    coarse, cell = places(count, place, parent[...], octant[...])
    table[...] = jnp.zeros_like(table)
    table[0:1, :] = cell.astype(F32)
    table[1:2, :] = coarse.astype(F32)
    table[2:3, :] = octant[...].astype(F32)
    fill_hot(own_hot, cell, 0)
    masks = edge_masks()
    lane = lax.broadcasted_iota(jnp.int32, (1, V), 1)
    named[...] = jnp.zeros_like(named)
    named[0:27, :] = EMPTY - nbr[...]
    named[27:28, :] = 2 * V - lane
    high, low = pieces(named[...])
    own = jnp.concatenate([feats[...], high.astype(BF16), low.astype(BF16)], axis=0)
    own = dot_nt(own, own_hot[...])
    wide[:, LAYER : LAYER + CELLS] = own[0:C].astype(BF16)
    told = own[C : C + 32] * 64.0 + own[C + 32 : C + 64]
    occupied = told[27:28] > 0.0
    ids[:, LAYER : LAYER + CELLS] = jnp.broadcast_to(told[27:28], (8, CELLS))

    for copy in marks:
        copy.wait()
    _, prev_cell = places(count, before, prev_p[...], prev_o[...])
    _, next_cell = places(count, after, next_p[...], next_o[...])
    prev_cell = jnp.where(place > 0, prev_cell, -1)
    next_cell = jnp.where(place < count - 1, next_cell, -1)
    edges[...] = jnp.zeros_like(edges)
    edges[0:1, 0:HALF] = prev_cell.astype(F32)
    edges[0:1, HALF:V] = next_cell.astype(F32)
    fill_hot(prev_hot, prev_cell, 3 * LAYER)
    fill_hot(next_hot, next_cell, 0)
    for copy in halos:
        copy.wait()
    row = lax.broadcasted_iota(jnp.int32, (16, HALF), 0)
    half_lane = lax.broadcasted_iota(jnp.int32, (16, HALF), 1)
    for edge, where_hot, names, at in (
        (prev_f, prev_hot, EMPTY - HALF - half_lane, 0),
        (next_f, next_hot, V - half_lane, LAYER + CELLS),
    ):
        high, low = pieces(names)
        tail = jnp.where(row == 0, high, jnp.where(row == 1, low, 0.0)).astype(BF16)
        placed = dot_nt(jnp.concatenate([edge[...], tail], axis=0), where_hot[...])
        wide[:, at : at + LAYER] = placed[0:C].astype(BF16)
        ids[:, at : at + LAYER] = jnp.broadcast_to(
            placed[C : C + 1] * 64.0 + placed[C + 1 : C + 2], (8, LAYER)
        )

    for tap in range(9):
        seen[tap * 8 : (tap + 1) * 8, :] = shifted(ids[...], tap, masks)
    row = lax.broadcasted_iota(jnp.int32, (8, CELLS), 0)
    worst = jnp.zeros((8, CELLS), F32)
    for group in range(4):
        expect = jnp.zeros((8, CELLS), F32)
        for k in range(group * 8, min(group * 8 + 8, 27)):
            layer, tap = k // 9, k % 9
            expect = jnp.where(
                row == k % 8, seen[tap * 8 : (tap + 1) * 8, layer * LAYER : layer * LAYER + CELLS], expect
            )
        differs = jnp.abs(told[group * 8 : group * 8 + 8] - expect)
        if group == 3:
            differs = jnp.where(row < 3, differs, 0.0)
        worst = jnp.maximum(worst, differs)
    worst = jnp.where(jnp.broadcast_to(occupied, (8, CELLS)), worst, 0.0)
    wrong[0] = jnp.maximum(jnp.max(worst), jnp.max(-cell.astype(F32)))

    unfold(wide, masks, taps)
    weights = jnp.concatenate([w_conv[:, d * TAPS : (d + 1) * TAPS] for d in range(3)], axis=0)
    spread[...] = dot(weights, taps[...])

    coarse_halo.wait()
    lookup[0:128, :] = prev_g[128:VC, :]
    lookup[128:VC, :] = grads[0:128, :]
    product = dot_nt(w_down[...], lookup[...])
    blocks = []
    for b in range(8):
        h, at = b // 2 % 2, b // 4 * 128 + b % 2 * C
        blocks.append(
            jnp.concatenate(
                [product[(h * 4 + q) * C : (h * 4 + q + 1) * C, at : at + C] for q in range(4)], axis=1
            )
        )
    high, low = split(jnp.concatenate(blocks, axis=0))
    spread_back = octant_order(True)
    rows = dot(high, spread_back) + dot(low, spread_back)
    for b in range(8):
        back[:, b * 256 : (b + 1) * 256] = rows[b * C : (b + 1) * C]

    middles = []
    for b in range(8):
        at = b * 256
        act = (
            spread[0:C, at : at + 256]
            + spread[C : 2 * C, LAYER + at : LAYER + at + 256]
            + spread[2 * C : 3 * C, 2 * LAYER + at : 2 * LAYER + at + 256]
        )
        here = jnp.broadcast_to(occupied[:, at : at + 256], (C, 256))
        gate = jax.nn.sigmoid(act)
        held = wide[:, LAYER + at : LAYER + at + 256].astype(F32)
        middles.append(jnp.where(here, held + act * gate, 0.0).astype(BF16))
        slope = back[:, at : at + 256] * gate * (1.0 + act * (1.0 - gate))
        slopes[:, at : at + 256] = jnp.where(here, slope, 0.0).astype(BF16)

    sorted_ = dot(jnp.concatenate(middles, axis=0), octant_order(False)).astype(BF16)
    children = jnp.concatenate(
        [
            jnp.concatenate(
                [
                    sorted_[b * C : (b + 1) * C, q * C : (q + 1) * C]
                    for b in (2 * h, 2 * h + 1, 4 + 2 * h, 5 + 2 * h)
                ],
                axis=1,
            )
            for h in range(2)
            for q in range(4)
        ],
        axis=0,
    )
    sums = dot_tn(children, w_down[...])
    coarse_prev[0:128, :] = jnp.zeros((128, C2), BF16)
    coarse_prev[128:VC, :] = sums[0:128].astype(BF16)
    coarse_own[0:128, :] = sums[128:VC]
    coarse_own[128:VC, :] = jnp.zeros((128, C2), F32)
    part_b[128:ROWS_B, :] = dot(children, lookup[...])

    turned = slopes[...].T
    stack[...] = jnp.zeros_like(stack)
    for d in range(3):
        stack[d * LAYER : d * LAYER + CELLS, d * C : (d + 1) * C] = turned
    product = dot(taps[...], stack[...])
    conv[:, 27 * C : 28 * C] = jnp.zeros((C, C), F32)
    conv[:, 0 : 27 * C] = jnp.concatenate([product[:, d * C : (d + 1) * C].T for d in range(3)], axis=1)
    store_conv(conv, part_a, part_b)
    grad_pre[...] = dot(slopes[...], own_hot[...]).astype(BF16)


def repair_kernel(
    wrong, feats, prev_f, next_f, table, nbr, w_conv, w_down, grads, prev_g,
    old_pre, old_a, old_b, old_own, old_prev,
    grad_pre, part_a, part_b, coarse_own, coarse_prev, back,
    feats_v, cand, table_v, nbr_v, conv_v, down_v, lookup, rows, preact, slope_v, back_v, conv, spread, parent_hot,
    part_a_v, part_b_v, own_v, prev_v,
):
    @pl.when(wrong[0] > 0.0)
    def _():
        for src, dst in (
            (feats, feats_v), (prev_f, cand.at[:, pl.ds(0, HALF)]), (feats, cand.at[:, pl.ds(HALF, V)]),
            (next_f, cand.at[:, pl.ds(HALF + V, HALF)]), (table, table_v), (nbr, nbr_v), (w_conv, conv_v),
            (w_down, down_v), (prev_g, lookup.at[pl.ds(0, VC)]), (grads, lookup.at[pl.ds(VC, VC)]),
        ):
            pltpu.sync_copy(src, dst)
        preact[...] = dot(conv_v[:, 26 * C : 27 * C], named_rows(nbr_v[26:27, :], rows, cand[...]))

        def forward(i, carry):
            block = conv_v[:, pl.ds(pl.multiple_of(i * 128, 128), 128)]
            for half in range(2):
                read = named_rows(nbr_v[pl.ds(2 * i + half, 1), :], rows, cand[...])
                preact[...] += dot(block[:, half * C : (half + 1) * C], read)
            return carry

        lax.fori_loop(0, 13, forward, 0)
        act = preact[...]
        gate = jax.nn.sigmoid(act)
        middle = feats_v[...].astype(F32) + act * gate
        fill_hot(parent_hot, table_v[1:2, :].astype(jnp.int32), 0)
        parent_grads = dot_tn(lookup[...], parent_hot[...]).astype(BF16)
        back_all = dot(down_v[...], parent_grads)
        octant = table_v[2:3, :]
        total = jnp.zeros((C, V), F32)
        for o in range(8):
            chosen = jnp.broadcast_to(octant == float(o), (C, V))
            total += jnp.where(chosen, back_all[o * C : (o + 1) * C], 0.0)
            spread[o * C : (o + 1) * C, :] = jnp.where(chosen, middle, 0.0).astype(BF16)
        back_v[...] = total
        children = dot_nt(spread[...], parent_hot[...]).astype(BF16)
        sums = dot_tn(children, down_v[...])
        prev_v[...] = sums[0:VC].astype(BF16)
        own_v[...] = sums[VC : 2 * VC]
        part_b_v[128:ROWS_B, :] = dot(children, lookup[...])
        slope_v[...] = (total * gate * (1.0 + act * (1.0 - gate))).astype(BF16)

        def weight(i, carry):
            both = [
                dot_nt(slope_v[...], named_rows(nbr_v[pl.ds(2 * i + half, 1), :], rows, cand[...]))
                for half in range(2)
            ]
            conv[:, pl.ds(pl.multiple_of(i * 128, 128), 128)] = jnp.concatenate(both, axis=1)
            return carry

        lax.fori_loop(0, 13, weight, 0)
        last = dot_nt(slope_v[...], named_rows(nbr_v[26:27, :], rows, cand[...]))
        conv[:, 26 * C : 28 * C] = jnp.concatenate([last, jnp.zeros_like(last)], axis=1)
        store_conv(conv, part_a_v, part_b_v)
        for src, dst in (
            (slope_v, grad_pre), (part_a_v, part_a), (part_b_v, part_b), (own_v, coarse_own),
            (prev_v, coarse_prev), (back_v, back),
        ):
            pltpu.sync_copy(src, dst)


def total_kernel(
    count, dims, grad_pre, slopes, back, coarse_own, coarse, table, edges, w_conv, part_a, part_b,
    prev_p, next_p, coarse_out, grad_feats, done,
    got_a1, got_b1, sum_a1, sum_b1, got_a2, got_b2, got_z, coarse_in,
    own_hot, prev_hot, next_hot, wide, taps, weights, spread,
    halo_send, halo_recv, send_a, recv_a, send_b, recv_b, send_z, recv_z, send_g, recv_g,
):
    nx, nz, ny = dims
    place = lax.axis_index("space")
    y, z, x = place % ny, place // ny % nz, place // (ny * nz)
    after, before = (place + 1) % count, (place + count - 1) % count
    ys = [peer(place, dims, "y", d) for d in range(1, ny)]
    xs = [peer(place, dims, "x", d) for d in range(1, nx)]
    zs = [peer(place, dims, "z", d) for d in range(1, nz)]
    greet([after, before] + ys + xs + zs)

    first = []
    for d in range(1, ny):
        first.append(
            push(part_a.at[(y + d) % ny], got_a1.at[d - 1], send_a.at[0, d - 1], recv_a.at[0, d - 1], ys[d - 1])
        )
    for d in range(1, nx):
        first.append(
            push(part_b.at[(x + d) % nx], got_b1.at[d - 1], send_b.at[0, d - 1], recv_b.at[0, d - 1], xs[d - 1])
        )
    halos = [
        push(grad_pre.at[:, pl.ds(HALF, HALF)], prev_p, halo_send.at[0], halo_recv.at[0], after),
        push(grad_pre.at[:, pl.ds(0, HALF)], next_p, halo_send.at[1], halo_recv.at[1], before),
        push(coarse, coarse_in, halo_send.at[2], halo_recv.at[2], before),
    ]

    fill_hot(own_hot, table[0:1, :].astype(jnp.int32), 0)
    fill_hot(prev_hot, edges[0:1, 0:HALF].astype(jnp.int32), 3 * LAYER)
    fill_hot(next_hot, edges[0:1, HALF:V].astype(jnp.int32), 0)
    for layer in range(3):
        for tap in range(9):
            k = 26 - (layer * 9 + tap)
            weights[tap * C : (tap + 1) * C, layer * C : (layer + 1) * C] = w_conv[:, k * C : (k + 1) * C]

    for copy in first:
        copy.wait()
    size_a, size_b = ROWS_A // (ny * nx), ROWS_B // (ny * nx)
    total = part_a[y]
    for d in range(ny - 1):
        total += got_a1[d]
    for i in range(nx):
        sum_a1[i] = total[i * size_a : (i + 1) * size_a]
    total = part_b[x]
    for d in range(nx - 1):
        total += got_b1[d]
    for i in range(ny):
        sum_b1[i] = total[i * size_b : (i + 1) * size_b]
    second = []
    for d in range(1, nx):
        second.append(
            push(sum_a1.at[(x + d) % nx], got_a2.at[d - 1], send_a.at[1, d - 1], recv_a.at[1, d - 1], xs[d - 1])
        )
    for d in range(1, ny):
        second.append(
            push(sum_b1.at[(y + d) % ny], got_b2.at[d - 1], send_b.at[1, d - 1], recv_b.at[1, d - 1], ys[d - 1])
        )

    for copy in halos:
        copy.wait()
    coarse_out[...] = (coarse_own[...] + coarse_in[...].astype(F32)).astype(BF16)
    wide[:, 0:LAYER] = dot_nt(prev_p[...], prev_hot[...]).astype(BF16)
    wide[:, LAYER : LAYER + CELLS] = slopes[...]
    wide[:, LAYER + CELLS : WIDE] = dot_nt(next_p[...], next_hot[...]).astype(BF16)
    unfold(wide, edge_masks(), taps)

    for copy in second:
        copy.wait()
    total = sum_a1[x]
    for d in range(nx - 1):
        total += got_a2[d]
    got_z[z, 0:size_a, :] = total
    total = sum_b1[y]
    for d in range(ny - 1):
        total += got_b2[d]
    got_z[z, size_a : size_a + size_b, :] = total

    third = [
        push(got_z.at[z], got_z.at[z], send_z.at[d - 1], recv_z.at[d - 1], zs[d - 1])
        for d in range(1, nz)
    ]

    spread[...] = dot_tn(weights[...], taps[...])
    cells = (
        spread[0:C, 0:CELLS]
        + spread[C : 2 * C, LAYER : LAYER + CELLS]
        + spread[2 * C : 3 * C, 2 * LAYER : 2 * LAYER + CELLS]
        + back[...]
    )
    both = dot(jnp.concatenate(split(cells), axis=0), own_hot[...])
    grad_feats[...] = (both[0:C] + both[C : 2 * C]).astype(BF16)

    for copy in third:
        copy.wait()
    total = got_z[0]
    for i in range(1, nz):
        total += got_z[i]
    done[x, y, 0, 0:size_a, :] = total[0:size_a].astype(BF16)
    done[x, y, 1, 0:size_b, :] = total[size_a : size_a + size_b].astype(BF16)

    fourth = [
        push(done.at[x, y, 0], done.at[x, y, 0], send_g.at[0, d - 1], recv_g.at[0, d - 1], xs[d - 1])
        for d in range(1, nx)
    ] + [
        push(done.at[x, y, 1], done.at[x, y, 1], send_g.at[1, d - 1], recv_g.at[1, d - 1], ys[d - 1])
        for d in range(1, ny)
    ]
    for copy in fourth:
        copy.wait()
    fifth = [
        push(done.at[:, y, 0], done.at[:, y, 0], send_g.at[2, d - 1], recv_g.at[2, d - 1], ys[d - 1])
        for d in range(1, ny)
    ] + [
        push(done.at[x, :, 1], done.at[x, :, 1], send_g.at[3, d - 1], recv_g.at[3, d - 1], xs[d - 1])
        for d in range(1, nx)
    ]
    for copy in fifth:
        copy.wait()


def finish_kernel(
    dims, scale, wrong, grad_fast, coarse, done, grad_pre, prev_p, next_p, nbr, w_conv, back,
    coarse_out, grad_feats, grad_conv, grad_down,
    flat, cand, nbr_v, conv_v, spill, rows,
):
    nx, _, ny = dims
    coarse_out[...] = coarse[...]
    grad_feats[...] = grad_fast[...]
    size_a, size_b = ROWS_A // (ny * nx), ROWS_B // (ny * nx)
    for i in range(nx):
        for j in range(ny):
            at = (j * nx + i) * size_a
            flat[at : at + size_a, :] = done[i, j, 0, 0:size_a, :].astype(F32) * scale
            at = ROWS_A + (i * ny + j) * size_b
            flat[at : at + size_b, :] = done[i, j, 1, 0:size_b, :].astype(F32) * scale
    for t in range(13):
        grad_conv[:, t * 128 : (t + 1) * 128] = flat[t * C : (t + 1) * C, :]
    grad_conv[:, 13 * 128 : 27 * C] = flat[13 * C : 14 * C, 0:C]
    grad_down[...] = flat[14 * C : 14 * C + 8 * C, :]

    @pl.when(wrong[0] > 0.0)
    def _():
        for src, dst in (
            (prev_p, cand.at[:, pl.ds(0, HALF)]), (grad_pre, cand.at[:, pl.ds(HALF, V)]),
            (next_p, cand.at[:, pl.ds(HALF + V, HALF)]), (nbr, nbr_v), (w_conv, conv_v), (back, spill),
        ):
            pltpu.sync_copy(src, dst)
        spill[...] += dot_tn(conv_v[:, 26 * C : 27 * C], named_rows(nbr_v[0:1, :], rows, cand[...]))

        def pull(i, carry):
            block = conv_v[:, pl.ds(pl.multiple_of(i * 128, 128), 128)]
            for half in range(2):
                read = named_rows(nbr_v[pl.ds(26 - 2 * i - half, 1), :], rows, cand[...])
                spill[...] += dot_tn(block[:, half * C : (half + 1) * C], read)
            return carry

        lax.fori_loop(0, 13, pull, 0)
        grad_feats[...] = spill[...].astype(BF16)


def vmem(n):
    return [pl.BlockSpec(memory_space=pltpu.VMEM)] * n


def anywhere(n):
    return [pl.BlockSpec(memory_space=pl.ANY)] * n


def shape(dims, dtype):
    return jax.ShapeDtypeStruct(dims, dtype)


GRANT = 32 * 1024 * 1024


def per_device(feats, w_conv, w_down, neighbors, parent, octant, grad_out):
    count = lax.axis_size("space")
    dims = CHIPS[count]
    nx, nz, ny = dims
    feats, w_conv = feats.T, w_conv.T
    parent, octant = parent.reshape(1, V), octant.reshape(1, V)
    dma = pltpu.SemaphoreType.DMA
    smem = [pl.BlockSpec(memory_space=pltpu.SMEM)]
    maps = [
        pltpu.VMEM((CELLS, V), BF16), pltpu.VMEM((LAYER, HALF), BF16), pltpu.VMEM((LAYER, HALF), BF16),
    ]
    half, row_half = shape((C, HALF), BF16), pltpu.VMEM((1, HALF), jnp.int32)

    (
        grad_pre, slopes, back, part_a, part_b, coarse_own, coarse_prev, wrong, table, edges,
        prev_f, next_f, prev_g,
    ) = pl.pallas_call(
        functools.partial(block_kernel, count),
        name="block",
        out_shape=(
            shape((C, V), BF16), shape((C, CELLS), BF16), shape((C, CELLS), F32),
            shape((ROWS_A, C2), F32), shape((ROWS_B, C2), F32), shape((VC, C2), F32), shape((VC, C2), BF16),
            shape((1,), F32), shape((8, V), F32), shape((8, V), F32), half, half, shape((VC, C2), BF16),
        ),
        in_specs=vmem(7),
        out_specs=tuple(vmem(7) + smem + vmem(5)),
        scratch_shapes=[row_half] * 4
        + maps
        + [
            pltpu.VMEM((C, WIDE), BF16), pltpu.VMEM((8, WIDE), F32), pltpu.VMEM((72, WIDE), F32),
            pltpu.VMEM((TAPS, WIDE), BF16), pltpu.VMEM((WIDE, 3 * C), BF16), pltpu.VMEM((32, V), jnp.int32),
            pltpu.VMEM((C, 28 * C), F32), pltpu.VMEM((3 * C, WIDE), F32), pltpu.VMEM((VC, C2), BF16),
            dma((7,)), dma((7,)),
        ],
        compiler_params=pltpu.CompilerParams(
            collective_id=0, has_side_effects=True, vmem_limit_bytes=GRANT
        ),
    )(feats, parent, octant, neighbors, w_conv, w_down, grad_out)

    grad_pre, part_a, part_b, coarse_own, coarse_prev, back_general = pl.pallas_call(
        repair_kernel,
        name="repair",
        out_shape=(
            shape((C, V), BF16), shape((ROWS_A, C2), F32), shape((ROWS_B, C2), F32),
            shape((VC, C2), F32), shape((VC, C2), BF16), shape((C, V), F32),
        ),
        in_specs=smem + anywhere(14),
        out_specs=tuple(anywhere(6)),
        input_output_aliases={10: 0, 11: 1, 12: 2, 13: 3, 14: 4},
        scratch_shapes=[
            pltpu.VMEM((C, V), BF16), pltpu.VMEM((C, 2 * V), BF16), pltpu.VMEM((8, V), F32),
            pltpu.VMEM((27, V), jnp.int32), pltpu.VMEM((C, 27 * C), BF16), pltpu.VMEM((8 * C, C2), BF16),
            pltpu.VMEM((2 * VC, C2), BF16), pltpu.VMEM((CELLS, V), BF16), pltpu.VMEM((C, V), F32),
            pltpu.VMEM((C, V), BF16), pltpu.VMEM((C, V), F32), pltpu.VMEM((C, 28 * C), F32),
            pltpu.VMEM((8 * C, V), BF16), pltpu.VMEM((2 * VC, V), BF16),
            pltpu.VMEM((ROWS_A, C2), F32), pltpu.VMEM((ROWS_B, C2), F32), pltpu.VMEM((VC, C2), F32),
            pltpu.VMEM((VC, C2), BF16),
        ],
        compiler_params=pltpu.CompilerParams(vmem_limit_bytes=GRANT),
    )(
        wrong, feats, prev_f, next_f, table, neighbors, w_conv, w_down, grad_out, prev_g,
        grad_pre, part_a, part_b, coarse_own, coarse_prev,
    )

    size_a, size_b = ROWS_A // (nx * ny), ROWS_B // (nx * ny)
    most = max(nx, ny) - 1
    prev_p, next_p, coarse_out, grad_feats, done = pl.pallas_call(
        functools.partial(total_kernel, count, dims),
        name="total",
        out_shape=(
            half, half, shape((VC, C2), BF16), shape((C, V), BF16), shape((nx, ny, 2, size_a, C2), BF16),
        ),
        in_specs=vmem(10),
        out_specs=tuple(vmem(5)),
        scratch_shapes=[
            pltpu.VMEM((ny - 1, ROWS_A // ny, C2), F32), pltpu.VMEM((nx - 1, ROWS_B // nx, C2), F32),
            pltpu.VMEM((nx, size_a, C2), F32), pltpu.VMEM((ny, size_b, C2), F32),
            pltpu.VMEM((nx - 1, size_a, C2), F32), pltpu.VMEM((ny - 1, size_b, C2), F32),
            pltpu.VMEM((nz, size_a + size_b, C2), F32), pltpu.VMEM((VC, C2), BF16),
        ]
        + maps
        + [
            pltpu.VMEM((C, WIDE), BF16), pltpu.VMEM((TAPS, WIDE), BF16), pltpu.VMEM((TAPS, 3 * C), BF16),
            pltpu.VMEM((3 * C, WIDE), F32),
            dma((3,)), dma((3,)), dma((2, most)), dma((2, most)), dma((2, most)), dma((2, most)),
            dma((nz - 1,)), dma((nz - 1,)), dma((4, most)), dma((4, most)),
        ],
        compiler_params=pltpu.CompilerParams(
            collective_id=1, has_side_effects=True, vmem_limit_bytes=GRANT
        ),
    )(
        grad_pre, slopes, back, coarse_own, coarse_prev, table, edges, w_conv,
        part_a.reshape(ny, ROWS_A // ny, C2), part_b.reshape(nx, ROWS_B // nx, C2),
    )

    coarse_out, grad_feats, grad_conv, grad_down = pl.pallas_call(
        functools.partial(finish_kernel, dims, 1.0 / math.sqrt(V * count)),
        name="finish",
        out_shape=(
            shape((VC, C2), BF16), shape((C, V), BF16), shape((C, 27 * C), F32), shape((8 * C, C2), F32),
        ),
        in_specs=smem + vmem(3) + anywhere(6),
        out_specs=tuple(vmem(4)),
        scratch_shapes=[
            pltpu.VMEM((ROWS_A + ROWS_B, C2), F32), pltpu.VMEM((C, 2 * V), BF16),
            pltpu.VMEM((27, V), jnp.int32), pltpu.VMEM((C, 27 * C), BF16), pltpu.VMEM((C, V), F32),
            pltpu.VMEM((CELLS, V), BF16),
        ],
        compiler_params=pltpu.CompilerParams(vmem_limit_bytes=GRANT),
    )(
        wrong, grad_feats, coarse_out, done, grad_pre, prev_p, next_p, neighbors, w_conv, back_general,
    )
    return coarse_out, grad_feats.T, grad_conv.T, grad_down


def solution(mesh):
    rows = P(("dp", "space"), None)
    line = P(("dp", "space"))
    return jax.shard_map(
        per_device,
        mesh=mesh,
        in_specs=(rows, P(), P(), P(None, ("dp", "space")), line, line, rows),
        out_specs=(rows, rows, P("dp", None), P("dp", None)),
        check_vma=False,
    )
```

time: 72.4 us -> 61.3 us (0.85)
  Pallas kernels: 70.1 us -> 54.4 us
  local copies, waits for them, and re-layouts: 0.74 us -> 5.86 us
    pallas_call x2, Pallas kernels: 27.5 us -> 19.6 us  [the longest x1 18.8 us: per_device(): pl.pallas_call(functools.partial(block_kernel, count), name='block', out_...]
    unnamed x4 -> x18, local copies, waits for them, and re-layouts: 0.66 us -> 5.86 us
    pallas_call x1, Pallas kernels: 6.68 us -> 1.62 us  [per_device(): pl.pallas_call(functools.partial(finish_kernel, dims, 1.0 / math.sqrt(V *...]
    pallas_call x1, Pallas kernels: 36 us -> 33.2 us  [per_device(): pl.pallas_call(functools.partial(total_kernel, count, dims), name='total'...]
where the time goes in v2:
time: 61.3 us; the launch traced here: 61 us
  Pallas kernels  54.4 us (89%)
  local copies, waits for them, and re-layouts  5.86 us (10%)
  between operations  0.69 us (1%)
    pallas_call x1, Pallas kernels, per_device(): pl.pallas_call(functools.partial(total_kernel, count, dims), name='total'...  33.2 us
    pallas_call x1, Pallas kernels, per_device(): pl.pallas_call(functools.partial(block_kernel, count), name='block', out_...  18.8 us
    unnamed x18, local copies, waits for them, and re-layouts  5.86 us
    pallas_call x1, Pallas kernels, per_device(): pl.pallas_call(functools.partial(finish_kernel, dims, 1.0 / math.sqrt(V *...  1.62 us

profile of v2, /device:TPU:8, one launch (start us, length us, event | category | flops | bytes accessed | tf_op | source)
XLA Modules:
  0.0 61.0 jit_solution(16878723650791815117)
XLA Ops:
  0.6 0.0 copy-start.7
  0.6 0.7 %copy-done.7 = s32[1024]{0:T(1024)S(1)} copy-done((s32[1024]{0:T(1024)S(1)}, s32[1024]{0:T(1024)}, u32[]{:S(2)}) %copy-start.7) | copy-done | bytes 4120
  1.3 0.0 copy-start
  1.3 0.9 %copy-done = bf16[1728,64]{0,1:T(8,128)(2,1)S(1)} copy-done((bf16[1728,64]{0,1:T(8,128)(2,1)S(1)}, bf16[1728,64]{0,1:T(8,128)(2,1)}, u32[]{:S(2)}) %copy-start) | copy-done | bytes 221208
  2.3 0.0 copy-start.2
  2.3 0.9 %copy-done.2 = s32[27,1024]{1,0:T(8,128)S(1)} copy-done((s32[27,1024]{1,0:T(8,128)S(1)}, s32[27,1024]{1,0:T(8,128)}, u32[]{:S(2)}) %copy-start.2) | copy-done | bytes 110616
  3.2 0.0 copy-start.3
  3.2 0.9 %copy-done.3 = bf16[1024,64]{0,1:T(8,128)(2,1)S(1)} copy-done((bf16[1024,64]{0,1:T(8,128)(2,1)S(1)}, bf16[1024,64]{0,1:T(8,128)(2,1)}, u32[]{:S(2)}) %copy-start.3) | copy-done | bytes 131096
  4.1 0.0 copy-start.4
  4.1 0.9 %copy-done.4 = bf16[512,128]{1,0:T(8,128)(2,1)S(1)} copy-done((bf16[512,128]{1,0:T(8,128)(2,1)S(1)}, bf16[512,128]{1,0:T(8,128)(2,1)}, u32[]{:S(2)}) %copy-start.4) | copy-done | bytes 131096
  5.0 0.0 copy-start.6
  5.0 0.8 %copy-done.6 = bf16[256,128]{1,0:T(8,128)(2,1)S(1)} copy-done((bf16[256,128]{1,0:T(8,128)(2,1)S(1)}, bf16[256,128]{1,0:T(8,128)(2,1)}, u32[]{:S(2)}) %copy-start.6) | copy-done | bytes 65560
  5.8 0.0 copy-start.8
  5.8 0.7 %copy-done.8 = s32[1024]{0:T(1024)S(1)} copy-done((s32[1024]{0:T(1024)S(1)}, s32[1024]{0:T(1024)}, u32[]{:S(2)}) %copy-start.8) | copy-done | bytes 4120
  6.5 0.0 copy-start.1
  6.5 0.0 copy-start.5
  6.5 18.8 %block.1 = (bf16[64,1024]{1,0:T(8,128)(2,1)S(1)}, bf16[64,2048]{1,0:T(8,128)(2,1)S(1)}, f32[64,2048]{1,0:T(8,128)S(1)}, f32[768,128]{1,0:T(8,128)S(1)}, f32[640,...) custom-call(bf16[64,1024]{1,0:T(8,128)(2,1)S(1)} %bitcast.14, ...), custom_call_target="tpu_custom_call" | custom-call | tf_op jit(solution)/shard_map/block/pallas_call | solution.py:573
  25.3 0.0 copy-done.1
  25.3 0.0 copy-done.5
  25.3 0.8 %repair.1 = (bf16[64,1024]{1,0:T(8,128)(2,1)S(1)}, f32[768,128]{1,0:T(8,128)S(1)}, f32[640,128]{1,0:T(8,128)S(1)}, f32[256,128]{1,0:T(8,128)S(1)}, bf16[256,128]{1,0:T(8,128)(2,1)S(1)}, /*index=5*/f32[64,1024]{1,0:T(8,128)S(1)}) custom-call(f32[1]{0:T(128)} %get-tuple-element.32.wrong, ...), custom_call_target="tpu_custom_call", output_to_operand_aliasing={{0}: (10, {}), {1}: (11, {}), {2}: (12, {}), {3}: (13, {}),... | custom-call | tf_op jit(solution)/shard_map/repair/pallas_call | solution.py:596
  26.2 33.2 %total.1 = (bf16[64,512]{1,0:T(8,128)(2,1)S(1)}, bf16[64,512]{1,0:T(8,128)(2,1)S(1)}, bf16[256,128]{1,0:T(8,128)(2,1)S(1)}, bf16[64,1024]{1,0:T(8,128)(2,1)S(1)}, bf16[4,4,2,48,128]{4,3,2,1,0:T(8,128)(2,1)S(1)}) custom-call(bf16[64,1024]{1,0:T(8,128)(2,1)S(1)} %get-tuple-element.42.grad_pre, bf16[64,2048]{1,0:T(8,128)(2,1)S(1)} %get-tuple-element.43.slopes, ...), custom_call_target="tpu_custom_call" | custom-call | tf_op jit(solution)/shard_map/total/pallas_call | solution.py:623
  59.4 1.6 %finish.1 = (bf16[256,128]{1,0:T(8,128)(2,1)}, bf16[64,1024]{1,0:T(8,128)(2,1)}, f32[64,1728]{1,0:T(8,128)}, f32[512,128]{1,0:T(8,128)}) custom-call(f32[1]{0:T(128)} %get-tuple-element.32.wrong, bf16[64,1024]{1,0:T(8,128)(2,1)S(1)} %get-tuple-element.50.grad_fast, bf16[256,128]{1,0:T(8,128)(2,1)S(1)} %get-tuple-element.51.coarse, ...), custom_call_target="tpu_custom_call" | custom-call | tf_op jit(solution)/shard_map/finish/pallas_call | solution.py:652
Async XLA Ops:
  0.6 0.7 %copy-start.7 = (s32[1024]{0:T(1024)S(1)}, s32[1024]{0:T(1024)}, u32[]{:S(2)}) copy-start(s32[1024]{0:T(1024)} %param.11) | copy-start | bytes 12292
  1.3 0.9 %copy-start = (bf16[1728,64]{0,1:T(8,128)(2,1)S(1)}, bf16[1728,64]{0,1:T(8,128)(2,1)}, u32[]{:S(2)}) copy-start(bf16[1728,64]{0,1:T(8,128)(2,1)} %param.8) | copy-start | bytes 663556
  2.3 0.9 %copy-start.2 = (s32[27,1024]{1,0:T(8,128)S(1)}, s32[27,1024]{1,0:T(8,128)}, u32[]{:S(2)}) copy-start(s32[27,1024]{1,0:T(8,128)} %nbr.5) | copy-start | bytes 331780
  3.2 0.9 %copy-start.3 = (bf16[1024,64]{0,1:T(8,128)(2,1)S(1)}, bf16[1024,64]{0,1:T(8,128)(2,1)}, u32[]{:S(2)}) copy-start(bf16[1024,64]{0,1:T(8,128)(2,1)} %param.7) | copy-start | bytes 393220
  4.1 0.9 %copy-start.4 = (bf16[512,128]{1,0:T(8,128)(2,1)S(1)}, bf16[512,128]{1,0:T(8,128)(2,1)}, u32[]{:S(2)}) copy-start(bf16[512,128]{1,0:T(8,128)(2,1)} %w_down.3) | copy-start | bytes 393220
  5.0 0.8 %copy-start.6 = (bf16[256,128]{1,0:T(8,128)(2,1)S(1)}, bf16[256,128]{1,0:T(8,128)(2,1)}, u32[]{:S(2)}) copy-start(bf16[256,128]{1,0:T(8,128)(2,1)} %grads.3) | copy-start | bytes 196612
  5.8 0.7 %copy-start.8 = (s32[1024]{0:T(1024)S(1)}, s32[1024]{0:T(1024)}, u32[]{:S(2)}) copy-start(s32[1024]{0:T(1024)} %param.12) | copy-start | bytes 12292
  6.5 18.8 %copy-start.1 = (bf16[1728,64]{0,1:T(8,128)(2,1)S(1)}, bf16[1728,64]{0,1:T(8,128)(2,1)}, u32[]{:S(2)}) copy-start(bf16[1728,64]{0,1:T(8,128)(2,1)} %param.8) | copy-start | bytes 663556
  6.5 18.8 %copy-start.5 = (bf16[512,128]{1,0:T(8,128)(2,1)S(1)}, bf16[512,128]{1,0:T(8,128)(2,1)}, u32[]{:S(2)}) copy-start(bf16[512,128]{1,0:T(8,128)(2,1)} %w_down.3) | copy-start | bytes 393220

commit v3 on v2

--- a/solution.py
+++ b/solution.py
@@ -60,13 +60,16 @@
     return place + ((x + step) % dims[0] - x) * (ny * nz)
 
 
-def greet(partners):
+def signal(partners):
     barrier = pltpu.get_barrier_semaphore()
     for other in partners:
         pl.semaphore_signal(
             barrier, inc=1, device_id={"space": other}, device_id_type=pl.DeviceIdType.MESH
         )
-    pl.semaphore_wait(barrier, len(partners))
+
+
+def await_partners(partners):
+    pl.semaphore_wait(pltpu.get_barrier_semaphore(), len(partners))
 
 
 def push(src, dst, send, recv, other):
@@ -155,15 +158,25 @@
 
 
 def block_kernel(
-    count, feats, parent, octant, nbr, w_conv, w_down, grads,
+    count, feats_in, parent_in, octant_in, nbr_in, w_conv_in, w_down_in, grads_in,
     grad_pre, slopes, back, part_a, part_b, coarse_own, coarse_prev, wrong, table, edges,
     prev_f, next_f, prev_g,
     prev_p, next_p, prev_o, next_o, own_hot, prev_hot, next_hot, wide, ids, seen, taps, stack, named,
-    conv, spread, lookup, send, recv,
+    conv, spread, lookup, feats, parent, octant, nbr, w_conv, w_down, grads, send, recv, load,
 ):
     place = lax.axis_index("space")
     after, before = (place + 1) % count, (place + count - 1) % count
-    greet((after, before))
+    signal((after, before))
+    inputs = (
+        (parent_in, parent), (octant_in, octant), (feats_in, feats), (grads_in, grads), (nbr_in, nbr),
+        (w_conv_in, w_conv), (w_down_in, w_down),
+    )
+    loads = [pltpu.make_async_copy(src, dst, load.at[i]) for i, (src, dst) in enumerate(inputs)]
+    for copy in loads:
+        copy.start()
+    for copy in loads[0:4]:
+        copy.wait()
+    await_partners((after, before))
     late, early = pl.ds(HALF, HALF), pl.ds(0, HALF)
     marks = [
         push(parent.at[:, late], prev_p, send.at[0], recv.at[0], after),
@@ -177,6 +190,8 @@
     ]
     coarse_halo = push(grads, prev_g, send.at[6], recv.at[6], after)
 
+    for copy in loads[4:]:
+        copy.wait()
     coarse, cell = places(count, place, parent[...], octant[...])
     table[...] = jnp.zeros_like(table)
     table[0:1, :] = cell.astype(F32)
@@ -389,7 +404,13 @@
     ys = [peer(place, dims, "y", d) for d in range(1, ny)]
     xs = [peer(place, dims, "x", d) for d in range(1, nx)]
     zs = [peer(place, dims, "z", d) for d in range(1, nz)]
-    greet([after, before] + ys + xs + zs)
+    partners = [after, before] + ys + xs + zs
+    signal(partners)
+
+    fill_hot(own_hot, table[0:1, :].astype(jnp.int32), 0)
+    fill_hot(prev_hot, edges[0:1, 0:HALF].astype(jnp.int32), 3 * LAYER)
+    fill_hot(next_hot, edges[0:1, HALF:V].astype(jnp.int32), 0)
+    await_partners(partners)
 
     first = []
     for d in range(1, ny):
@@ -406,9 +427,6 @@
         push(coarse, coarse_in, halo_send.at[2], halo_recv.at[2], before),
     ]
 
-    fill_hot(own_hot, table[0:1, :].astype(jnp.int32), 0)
-    fill_hot(prev_hot, edges[0:1, 0:HALF].astype(jnp.int32), 3 * LAYER)
-    fill_hot(next_hot, edges[0:1, HALF:V].astype(jnp.int32), 0)
     for layer in range(3):
         for tap in range(9):
             k = 26 - (layer * 9 + tap)
@@ -559,7 +577,13 @@
     dims = CHIPS[count]
     nx, nz, ny = dims
     feats, w_conv = feats.T, w_conv.T
-    parent, octant = parent.reshape(1, V), octant.reshape(1, V)
+    weights = w_conv
+    feats, parent, octant, neighbors, w_conv, w_down, grad_out = (
+        pltpu.with_memory_space_constraint(x, pltpu.HBM)
+        for x in (
+            feats, parent.reshape(1, V), octant.reshape(1, V), neighbors, w_conv, w_down, grad_out,
+        )
+    )
     dma = pltpu.SemaphoreType.DMA
     smem = [pl.BlockSpec(memory_space=pltpu.SMEM)]
     maps = [
@@ -578,7 +602,7 @@
             shape((ROWS_A, C2), F32), shape((ROWS_B, C2), F32), shape((VC, C2), F32), shape((VC, C2), BF16),
             shape((1,), F32), shape((8, V), F32), shape((8, V), F32), half, half, shape((VC, C2), BF16),
         ),
-        in_specs=vmem(7),
+        in_specs=[pl.BlockSpec(memory_space=pltpu.HBM)] * 7,
         out_specs=tuple(vmem(7) + smem + vmem(5)),
         scratch_shapes=[row_half] * 4
         + maps
@@ -586,7 +610,10 @@
             pltpu.VMEM((C, WIDE), BF16), pltpu.VMEM((8, WIDE), F32), pltpu.VMEM((72, WIDE), F32),
             pltpu.VMEM((TAPS, WIDE), BF16), pltpu.VMEM((WIDE, 3 * C), BF16), pltpu.VMEM((32, V), jnp.int32),
             pltpu.VMEM((C, 28 * C), F32), pltpu.VMEM((3 * C, WIDE), F32), pltpu.VMEM((VC, C2), BF16),
-            dma((7,)), dma((7,)),
+            pltpu.VMEM((C, V), BF16), pltpu.VMEM((1, V), jnp.int32), pltpu.VMEM((1, V), jnp.int32),
+            pltpu.VMEM((27, V), jnp.int32), pltpu.VMEM((C, 27 * C), BF16), pltpu.VMEM((8 * C, C2), BF16),
+            pltpu.VMEM((VC, C2), BF16),
+            dma((7,)), dma((7,)), dma((7,)),
         ],
         compiler_params=pltpu.CompilerParams(
             collective_id=0, has_side_effects=True, vmem_limit_bytes=GRANT
@@ -645,7 +672,7 @@
             collective_id=1, has_side_effects=True, vmem_limit_bytes=GRANT
         ),
     )(
-        grad_pre, slopes, back, coarse_own, coarse_prev, table, edges, w_conv,
+        grad_pre, slopes, back, coarse_own, coarse_prev, table, edges, weights,
         part_a.reshape(ny, ROWS_A // ny, C2), part_b.reshape(nx, ROWS_B // nx, C2),
     )
 

time: 61.3 us -> 55.5 us (0.905)
  local copies, waits for them, and re-layouts: 5.86 us -> 0.08 us
    unnamed x18 -> x2, local copies, waits for them, and re-layouts: 5.86 us -> 0.08 us
where the time goes in v3:
time: 55.5 us; the launch traced here: 55.3 us
  Pallas kernels  54.6 us (98%)
  between operations  0.66 us (1%)
    pallas_call x1, Pallas kernels, per_device(): pl.pallas_call(functools.partial(total_kernel, count, dims), name='total'...  33.1 us
    pallas_call x1, Pallas kernels, per_device(): pl.pallas_call(functools.partial(block_kernel, count), name='block', out_...  19 us
    pallas_call x1, Pallas kernels, per_device(): pl.pallas_call(functools.partial(finish_kernel, dims, 1.0 / math.sqrt(V *...  1.61 us

profile of v3, /device:TPU:8, one launch (start us, length us, event | category | flops | bytes accessed | tf_op | source)
XLA Modules:
  0.0 55.3 jit_solution(11894616558451972151)
XLA Ops:
  0.6 19.0 %block.1 = (bf16[64,1024]{1,0:T(8,128)(2,1)S(1)}, bf16[64,2048]{1,0:T(8,128)(2,1)S(1)}, f32[64,2048]{1,0:T(8,128)S(1)}, f32[768,128]{1,0:T(8,128)S(1)}, f32[640,...) custom-call(bf16[64,1024]{1,0:T(8,128)(2,1)} %bitcast.14, ...), custom_call_target="tpu_custom_call" | custom-call | tf_op jit(solution)/shard_map/block/pallas_call | solution.py:597
  19.6 0.0 copy-start
  19.6 0.8 %repair.1 = (bf16[64,1024]{1,0:T(8,128)(2,1)S(1)}, f32[768,128]{1,0:T(8,128)S(1)}, f32[640,128]{1,0:T(8,128)S(1)}, f32[256,128]{1,0:T(8,128)S(1)}, bf16[256,128]{1,0:T(8,128)(2,1)S(1)}, /*index=5*/f32[64,1024]{1,0:T(8,128)S(1)}) custom-call(f32[1]{0:T(128)} %get-tuple-element.32.wrong, ...), custom_call_target="tpu_custom_call", output_to_operand_aliasing={{0}: (10, {}), {1}: (11, {}), {2}: (12, {}), {3}: (13, {}),... | custom-call | tf_op jit(solution)/shard_map/repair/pallas_call | solution.py:623
  20.5 0.1 copy-done
  20.6 33.1 %total.1 = (bf16[64,512]{1,0:T(8,128)(2,1)S(1)}, bf16[64,512]{1,0:T(8,128)(2,1)S(1)}, bf16[256,128]{1,0:T(8,128)(2,1)S(1)}, bf16[64,1024]{1,0:T(8,128)(2,1)S(1)}, bf16[4,4,2,48,128]{4,3,2,1,0:T(8,128)(2,1)S(1)}) custom-call(bf16[64,1024]{1,0:T(8,128)(2,1)S(1)} %get-tuple-element.42.grad_pre, bf16[64,2048]{1,0:T(8,128)(2,1)S(1)} %get-tuple-element.43.slopes, ...), custom_call_target="tpu_custom_call" | custom-call | tf_op jit(solution)/shard_map/total/pallas_call | solution.py:650
  53.7 1.6 %finish.1 = (bf16[256,128]{1,0:T(8,128)(2,1)}, bf16[64,1024]{1,0:T(8,128)(2,1)}, f32[64,1728]{1,0:T(8,128)}, f32[512,128]{1,0:T(8,128)}) custom-call(f32[1]{0:T(128)} %get-tuple-element.32.wrong, bf16[64,1024]{1,0:T(8,128)(2,1)S(1)} %get-tuple-element.50.grad_fast, bf16[256,128]{1,0:T(8,128)(2,1)S(1)} %get-tuple-element.51.coarse, ...), custom_call_target="tpu_custom_call" | custom-call | tf_op jit(solution)/shard_map/finish/pallas_call | solution.py:679
Async XLA Ops:
  19.6 0.9 %copy-start = (bf16[1728,64]{0,1:T(8,128)(2,1)S(1)}, bf16[1728,64]{0,1:T(8,128)(2,1)}, u32[]{:S(2)}) copy-start(bf16[1728,64]{0,1:T(8,128)(2,1)} %param.8) | copy-start | bytes 663556

commit v4 on v3

--- a/solution.py
+++ b/solution.py
@@ -21,8 +21,9 @@
 WIDE = CELLS + 2 * LAYER
 EMPTY = 3 * V
 TAPS = 9 * C
-ROWS_A, ROWS_B = 768, 640
-CHIPS = {128: (4, 8, 4), 16: (2, 2, 4)}
+SUMS = 22 * C
+CHUNK = 96
+CHIPS = {128: (4, 8, 4)}
 
 
 def dot(a, b):
@@ -47,6 +48,21 @@
     for t in range(ref.shape[0] // 16):
         ref[t * 16 : (t + 1) * 16, :] = jnp.where(
             high == jnp.asarray(first // 16 + t, BF16), low, none
+        )
+
+
+def fill_hot_t(ref, ids, first):
+    count = ids.shape[1]
+    high, low = lax.shift_right_arithmetic(ids, 7).astype(F32), (ids & 127).astype(F32)
+    row = lax.broadcasted_iota(jnp.int32, (8, count), 0)
+    columns = jnp.where(row == 0, jnp.broadcast_to(high, row.shape), jnp.broadcast_to(low, row.shape)).T
+    lane = lax.broadcasted_iota(jnp.int32, (count, 128), 1).astype(F32)
+    high = jnp.broadcast_to(columns[:, 0:1], lane.shape).astype(BF16)
+    low = jnp.where(jnp.broadcast_to(columns[:, 1:2], lane.shape) == lane, 1.0, 0.0).astype(BF16)
+    none = jnp.zeros_like(low)
+    for t in range(ref.shape[1] // 128):
+        ref[:, t * 128 : (t + 1) * 128] = jnp.where(
+            high == jnp.asarray(first // 128 + t, BF16), low, none
         )
 
 
@@ -150,16 +166,15 @@
     return jnp.where(cell == y * SZ + z, 1.0, 0.0).astype(BF16)
 
 
-def store_conv(conv, part_a, part_b):
-    for t in range(12):
-        part_a[t * C : (t + 1) * C, :] = conv[:, t * 128 : (t + 1) * 128]
-    for t in range(2):
-        part_b[t * C : (t + 1) * C, :] = conv[:, (12 + t) * 128 : (13 + t) * 128]
+def store_conv(conv, sums):
+    for t in range(14):
+        sums[t * C : (t + 1) * C, :] = conv[:, t * 128 : (t + 1) * 128].astype(BF16)
+    sums[SUMS : sums.shape[0], :] = jnp.zeros((sums.shape[0] - SUMS, C2), BF16)
 
 
 def block_kernel(
     count, feats_in, parent_in, octant_in, nbr_in, w_conv_in, w_down_in, grads_in,
-    grad_pre, slopes, back, part_a, part_b, coarse_own, coarse_prev, wrong, table, edges,
+    slopes, back, sums, coarse_own, coarse_prev, wrong, table, edges,
     prev_f, next_f, prev_g,
     prev_p, next_p, prev_o, next_o, own_hot, prev_hot, next_hot, wide, ids, seen, taps, stack, named,
     conv, spread, lookup, feats, parent, octant, nbr, w_conv, w_down, grads, send, recv, load,
@@ -197,7 +212,7 @@
     table[0:1, :] = cell.astype(F32)
     table[1:2, :] = coarse.astype(F32)
     table[2:3, :] = octant[...].astype(F32)
-    fill_hot(own_hot, cell, 0)
+    fill_hot_t(own_hot, cell, 0)
     masks = edge_masks()
     lane = lax.broadcasted_iota(jnp.int32, (1, V), 1)
     named[...] = jnp.zeros_like(named)
@@ -205,7 +220,7 @@
     named[27:28, :] = 2 * V - lane
     high, low = pieces(named[...])
     own = jnp.concatenate([feats[...], high.astype(BF16), low.astype(BF16)], axis=0)
-    own = dot_nt(own, own_hot[...])
+    own = dot(own, own_hot[...])
     wide[:, LAYER : LAYER + CELLS] = own[0:C].astype(BF16)
     told = own[C : C + 32] * 64.0 + own[C + 32 : C + 64]
     occupied = told[27:28] > 0.0
@@ -220,8 +235,8 @@
     edges[...] = jnp.zeros_like(edges)
     edges[0:1, 0:HALF] = prev_cell.astype(F32)
     edges[0:1, HALF:V] = next_cell.astype(F32)
-    fill_hot(prev_hot, prev_cell, 3 * LAYER)
-    fill_hot(next_hot, next_cell, 0)
+    fill_hot_t(prev_hot, prev_cell, 3 * LAYER)
+    fill_hot_t(next_hot, next_cell, 0)
     for copy in halos:
         copy.wait()
     row = lax.broadcasted_iota(jnp.int32, (16, HALF), 0)
@@ -232,7 +247,7 @@
     ):
         high, low = pieces(names)
         tail = jnp.where(row == 0, high, jnp.where(row == 1, low, 0.0)).astype(BF16)
-        placed = dot_nt(jnp.concatenate([edge[...], tail], axis=0), where_hot[...])
+        placed = dot(jnp.concatenate([edge[...], tail], axis=0), where_hot[...])
         wide[:, at : at + LAYER] = placed[0:C].astype(BF16)
         ids[:, at : at + LAYER] = jnp.broadcast_to(
             placed[C : C + 1] * 64.0 + placed[C + 1 : C + 2], (8, LAYER)
@@ -308,12 +323,12 @@
         ],
         axis=0,
     )
-    sums = dot_tn(children, w_down[...])
+    coarse = dot_tn(children, w_down[...])
     coarse_prev[0:128, :] = jnp.zeros((128, C2), BF16)
-    coarse_prev[128:VC, :] = sums[0:128].astype(BF16)
-    coarse_own[0:128, :] = sums[128:VC]
+    coarse_prev[128:VC, :] = coarse[0:128].astype(BF16)
+    coarse_own[0:128, :] = coarse[128:VC]
     coarse_own[128:VC, :] = jnp.zeros((128, C2), F32)
-    part_b[128:ROWS_B, :] = dot(children, lookup[...])
+    sums[14 * C : SUMS, :] = dot(children, lookup[...]).astype(BF16)
 
     turned = slopes[...].T
     stack[...] = jnp.zeros_like(stack)
@@ -322,16 +337,15 @@
     product = dot(taps[...], stack[...])
     conv[:, 27 * C : 28 * C] = jnp.zeros((C, C), F32)
     conv[:, 0 : 27 * C] = jnp.concatenate([product[:, d * C : (d + 1) * C].T for d in range(3)], axis=1)
-    store_conv(conv, part_a, part_b)
-    grad_pre[...] = dot(slopes[...], own_hot[...]).astype(BF16)
+    store_conv(conv, sums)
 
 
 def repair_kernel(
     wrong, feats, prev_f, next_f, table, nbr, w_conv, w_down, grads, prev_g,
-    old_pre, old_a, old_b, old_own, old_prev,
-    grad_pre, part_a, part_b, coarse_own, coarse_prev, back,
+    old_sums, old_own, old_prev,
+    sums, coarse_own, coarse_prev, grad_pre, back,
     feats_v, cand, table_v, nbr_v, conv_v, down_v, lookup, rows, preact, slope_v, back_v, conv, spread, parent_hot,
-    part_a_v, part_b_v, own_v, prev_v,
+    sums_v, own_v, prev_v,
 ):
     @pl.when(wrong[0] > 0.0)
     def _():
@@ -365,10 +379,10 @@
             spread[o * C : (o + 1) * C, :] = jnp.where(chosen, middle, 0.0).astype(BF16)
         back_v[...] = total
         children = dot_nt(spread[...], parent_hot[...]).astype(BF16)
-        sums = dot_tn(children, down_v[...])
-        prev_v[...] = sums[0:VC].astype(BF16)
-        own_v[...] = sums[VC : 2 * VC]
-        part_b_v[128:ROWS_B, :] = dot(children, lookup[...])
+        coarse = dot_tn(children, down_v[...])
+        prev_v[...] = coarse[0:VC].astype(BF16)
+        own_v[...] = coarse[VC : 2 * VC]
+        sums_v[14 * C : SUMS, :] = dot(children, lookup[...]).astype(BF16)
         slope_v[...] = (total * gate * (1.0 + act * (1.0 - gate))).astype(BF16)
 
         def weight(i, carry):
@@ -382,101 +396,82 @@
         lax.fori_loop(0, 13, weight, 0)
         last = dot_nt(slope_v[...], named_rows(nbr_v[26:27, :], rows, cand[...]))
         conv[:, 26 * C : 28 * C] = jnp.concatenate([last, jnp.zeros_like(last)], axis=1)
-        store_conv(conv, part_a_v, part_b_v)
+        store_conv(conv, sums_v)
         for src, dst in (
-            (slope_v, grad_pre), (part_a_v, part_a), (part_b_v, part_b), (own_v, coarse_own),
-            (prev_v, coarse_prev), (back_v, back),
+            (slope_v, grad_pre), (sums_v, sums), (own_v, coarse_own), (prev_v, coarse_prev), (back_v, back),
         ):
             pltpu.sync_copy(src, dst)
 
 
 def total_kernel(
-    count, dims, grad_pre, slopes, back, coarse_own, coarse, table, edges, w_conv, part_a, part_b,
+    count, dims, wrong, general, slopes, back, coarse_own, coarse, table, edges, w_conv, sums,
     prev_p, next_p, coarse_out, grad_feats, done,
-    got_a1, got_b1, sum_a1, sum_b1, got_a2, got_b2, got_z, coarse_in,
-    own_hot, prev_hot, next_hot, wide, taps, weights, spread,
-    halo_send, halo_recv, send_a, recv_a, send_b, recv_b, send_z, recv_z, send_g, recv_g,
+    got, got_z, coarse_in, grad_pre, own_hot, prev_hot, next_hot, wide, taps, weights, spread,
+    halo_send, halo_recv, send, recv, send_z, recv_z, send_g, recv_g,
 ):
     nx, nz, ny = dims
     place = lax.axis_index("space")
     y, z, x = place % ny, place // ny % nz, place // (ny * nz)
+    mine = x * ny + y
     after, before = (place + 1) % count, (place + count - 1) % count
-    ys = [peer(place, dims, "y", d) for d in range(1, ny)]
-    xs = [peer(place, dims, "x", d) for d in range(1, nx)]
-    zs = [peer(place, dims, "z", d) for d in range(1, nz)]
-    partners = [after, before] + ys + xs + zs
+    steps = [(dx, dy) for dx in range(nx) for dy in range(ny)][1:]
+    plane = [peer(peer(place, dims, "x", dx), dims, "y", dy) for dx, dy in steps]
+    column = [peer(place, dims, "z", d) for d in range(1, nz)]
+    partners = [after, before] + plane + column
     signal(partners)
 
     fill_hot(own_hot, table[0:1, :].astype(jnp.int32), 0)
-    fill_hot(prev_hot, edges[0:1, 0:HALF].astype(jnp.int32), 3 * LAYER)
-    fill_hot(next_hot, edges[0:1, HALF:V].astype(jnp.int32), 0)
+    fill_hot_t(prev_hot, edges[0:1, 0:HALF].astype(jnp.int32), 3 * LAYER)
+    fill_hot_t(next_hot, edges[0:1, HALF:V].astype(jnp.int32), 0)
     await_partners(partners)
 
-    first = []
-    for d in range(1, ny):
-        first.append(
-            push(part_a.at[(y + d) % ny], got_a1.at[d - 1], send_a.at[0, d - 1], recv_a.at[0, d - 1], ys[d - 1])
-        )
-    for d in range(1, nx):
-        first.append(
-            push(part_b.at[(x + d) % nx], got_b1.at[d - 1], send_b.at[0, d - 1], recv_b.at[0, d - 1], xs[d - 1])
-        )
+    first = [
+        push(sums.at[(x + dx) % nx * ny + (y + dy) % ny], got.at[i], send.at[i], recv.at[i], plane[i])
+        for i, (dx, dy) in enumerate(steps)
+    ]
+
+    fast = dot(slopes[...], own_hot[...])
+    repaired = jnp.broadcast_to(wrong[0], fast.shape) > 0.0
+    grad_pre[...] = jnp.where(repaired, general[...].astype(F32), fast).astype(BF16)
+    for layer in range(3):
+        for tap in range(9):
+            k = 26 - (layer * 9 + tap)
+            weights[tap * C : (tap + 1) * C, layer * C : (layer + 1) * C] = w_conv[:, k * C : (k + 1) * C]
+
+    for copy in first:
+        copy.wait()
     halos = [
         push(grad_pre.at[:, pl.ds(HALF, HALF)], prev_p, halo_send.at[0], halo_recv.at[0], after),
         push(grad_pre.at[:, pl.ds(0, HALF)], next_p, halo_send.at[1], halo_recv.at[1], before),
         push(coarse, coarse_in, halo_send.at[2], halo_recv.at[2], before),
     ]
-
-    for layer in range(3):
-        for tap in range(9):
-            k = 26 - (layer * 9 + tap)
-            weights[tap * C : (tap + 1) * C, layer * C : (layer + 1) * C] = w_conv[:, k * C : (k + 1) * C]
-
-    for copy in first:
-        copy.wait()
-    size_a, size_b = ROWS_A // (ny * nx), ROWS_B // (ny * nx)
-    total = part_a[y]
-    for d in range(ny - 1):
-        total += got_a1[d]
-    for i in range(nx):
-        sum_a1[i] = total[i * size_a : (i + 1) * size_a]
-    total = part_b[x]
-    for d in range(nx - 1):
-        total += got_b1[d]
-    for i in range(ny):
-        sum_b1[i] = total[i * size_b : (i + 1) * size_b]
-    second = []
-    for d in range(1, nx):
-        second.append(
-            push(sum_a1.at[(x + d) % nx], got_a2.at[d - 1], send_a.at[1, d - 1], recv_a.at[1, d - 1], xs[d - 1])
-        )
-    for d in range(1, ny):
-        second.append(
-            push(sum_b1.at[(y + d) % ny], got_b2.at[d - 1], send_b.at[1, d - 1], recv_b.at[1, d - 1], ys[d - 1])
-        )
+    total = sums[mine].astype(F32)
+    for i in range(len(steps)):
+        total += got[i].astype(F32)
+    got_z[z] = total.astype(BF16)
+
+    second = [
+        push(got_z.at[z], got_z.at[z], send_z.at[d - 1], recv_z.at[d - 1], column[d - 1])
+        for d in range(1, nz)
+    ]
 
     for copy in halos:
         copy.wait()
     coarse_out[...] = (coarse_own[...] + coarse_in[...].astype(F32)).astype(BF16)
-    wide[:, 0:LAYER] = dot_nt(prev_p[...], prev_hot[...]).astype(BF16)
+    wide[:, 0:LAYER] = dot(prev_p[...], prev_hot[...]).astype(BF16)
     wide[:, LAYER : LAYER + CELLS] = slopes[...]
-    wide[:, LAYER + CELLS : WIDE] = dot_nt(next_p[...], next_hot[...]).astype(BF16)
+    wide[:, LAYER + CELLS : WIDE] = dot(next_p[...], next_hot[...]).astype(BF16)
     unfold(wide, edge_masks(), taps)
 
     for copy in second:
         copy.wait()
-    total = sum_a1[x]
-    for d in range(nx - 1):
-        total += got_a2[d]
-    got_z[z, 0:size_a, :] = total
-    total = sum_b1[y]
-    for d in range(ny - 1):
-        total += got_b2[d]
-    got_z[z, size_a : size_a + size_b, :] = total
+    total = got_z[0].astype(F32)
+    for i in range(1, nz):
+        total += got_z[i].astype(F32)
+    done[mine] = total.astype(BF16)
 
     third = [
-        push(got_z.at[z], got_z.at[z], send_z.at[d - 1], recv_z.at[d - 1], zs[d - 1])
-        for d in range(1, nz)
+        push(done.at[mine], done.at[mine], send_g.at[i], recv_g.at[i], plane[i]) for i in range(len(steps))
     ]
 
     spread[...] = dot_tn(weights[...], taps[...])
@@ -488,54 +483,21 @@
     )
     both = dot(jnp.concatenate(split(cells), axis=0), own_hot[...])
     grad_feats[...] = (both[0:C] + both[C : 2 * C]).astype(BF16)
-
     for copy in third:
         copy.wait()
-    total = got_z[0]
-    for i in range(1, nz):
-        total += got_z[i]
-    done[x, y, 0, 0:size_a, :] = total[0:size_a].astype(BF16)
-    done[x, y, 1, 0:size_b, :] = total[size_a : size_a + size_b].astype(BF16)
-
-    fourth = [
-        push(done.at[x, y, 0], done.at[x, y, 0], send_g.at[0, d - 1], recv_g.at[0, d - 1], xs[d - 1])
-        for d in range(1, nx)
-    ] + [
-        push(done.at[x, y, 1], done.at[x, y, 1], send_g.at[1, d - 1], recv_g.at[1, d - 1], ys[d - 1])
-        for d in range(1, ny)
-    ]
-    for copy in fourth:
-        copy.wait()
-    fifth = [
-        push(done.at[:, y, 0], done.at[:, y, 0], send_g.at[2, d - 1], recv_g.at[2, d - 1], ys[d - 1])
-        for d in range(1, ny)
-    ] + [
-        push(done.at[x, :, 1], done.at[x, :, 1], send_g.at[3, d - 1], recv_g.at[3, d - 1], xs[d - 1])
-        for d in range(1, nx)
-    ]
-    for copy in fifth:
-        copy.wait()
 
 
 def finish_kernel(
-    dims, scale, wrong, grad_fast, coarse, done, grad_pre, prev_p, next_p, nbr, w_conv, back,
+    scale, wrong, grad_fast, coarse, done, grad_pre, prev_p, next_p, nbr, w_conv, back,
     coarse_out, grad_feats, grad_conv, grad_down,
-    flat, cand, nbr_v, conv_v, spill, rows,
+    cand, nbr_v, conv_v, spill, rows,
 ):
-    nx, _, ny = dims
     coarse_out[...] = coarse[...]
     grad_feats[...] = grad_fast[...]
-    size_a, size_b = ROWS_A // (ny * nx), ROWS_B // (ny * nx)
-    for i in range(nx):
-        for j in range(ny):
-            at = (j * nx + i) * size_a
-            flat[at : at + size_a, :] = done[i, j, 0, 0:size_a, :].astype(F32) * scale
-            at = ROWS_A + (i * ny + j) * size_b
-            flat[at : at + size_b, :] = done[i, j, 1, 0:size_b, :].astype(F32) * scale
     for t in range(13):
-        grad_conv[:, t * 128 : (t + 1) * 128] = flat[t * C : (t + 1) * C, :]
-    grad_conv[:, 13 * 128 : 27 * C] = flat[13 * C : 14 * C, 0:C]
-    grad_down[...] = flat[14 * C : 14 * C + 8 * C, :]
+        grad_conv[:, t * 128 : (t + 1) * 128] = done[t * C : (t + 1) * C, :].astype(F32) * scale
+    grad_conv[:, 13 * 128 : 27 * C] = done[13 * C : 14 * C, 0:C].astype(F32) * scale
+    grad_down[...] = done[14 * C : SUMS, :].astype(F32) * scale
 
     @pl.when(wrong[0] > 0.0)
     def _():
@@ -589,23 +551,24 @@
     maps = [
         pltpu.VMEM((CELLS, V), BF16), pltpu.VMEM((LAYER, HALF), BF16), pltpu.VMEM((LAYER, HALF), BF16),
     ]
+    maps_t = [pltpu.VMEM((V, CELLS), BF16)] + maps[1:]
     half, row_half = shape((C, HALF), BF16), pltpu.VMEM((1, HALF), jnp.int32)
+    padded = shape((nx * ny * CHUNK, C2), BF16)
 
     (
-        grad_pre, slopes, back, part_a, part_b, coarse_own, coarse_prev, wrong, table, edges,
-        prev_f, next_f, prev_g,
+        slopes, back, sums, coarse_own, coarse_prev, wrong, table, edges, prev_f, next_f, prev_g,
     ) = pl.pallas_call(
         functools.partial(block_kernel, count),
         name="block",
         out_shape=(
-            shape((C, V), BF16), shape((C, CELLS), BF16), shape((C, CELLS), F32),
-            shape((ROWS_A, C2), F32), shape((ROWS_B, C2), F32), shape((VC, C2), F32), shape((VC, C2), BF16),
+            shape((C, CELLS), BF16), shape((C, CELLS), F32), padded,
+            shape((VC, C2), F32), shape((VC, C2), BF16),
             shape((1,), F32), shape((8, V), F32), shape((8, V), F32), half, half, shape((VC, C2), BF16),
         ),
         in_specs=[pl.BlockSpec(memory_space=pltpu.HBM)] * 7,
-        out_specs=tuple(vmem(7) + smem + vmem(5)),
+        out_specs=tuple(vmem(5) + smem + vmem(5)),
         scratch_shapes=[row_half] * 4
-        + maps
+        + maps_t
         + [
             pltpu.VMEM((C, WIDE), BF16), pltpu.VMEM((8, WIDE), F32), pltpu.VMEM((72, WIDE), F32),
             pltpu.VMEM((TAPS, WIDE), BF16), pltpu.VMEM((WIDE, 3 * C), BF16), pltpu.VMEM((32, V), jnp.int32),
@@ -620,64 +583,58 @@
         ),
     )(feats, parent, octant, neighbors, w_conv, w_down, grad_out)
 
-    grad_pre, part_a, part_b, coarse_own, coarse_prev, back_general = pl.pallas_call(
+    sums, coarse_own, coarse_prev, general, back_general = pl.pallas_call(
         repair_kernel,
         name="repair",
         out_shape=(
-            shape((C, V), BF16), shape((ROWS_A, C2), F32), shape((ROWS_B, C2), F32),
-            shape((VC, C2), F32), shape((VC, C2), BF16), shape((C, V), F32),
+            padded, shape((VC, C2), F32), shape((VC, C2), BF16), shape((C, V), BF16), shape((C, V), F32),
         ),
-        in_specs=smem + anywhere(14),
-        out_specs=tuple(anywhere(6)),
-        input_output_aliases={10: 0, 11: 1, 12: 2, 13: 3, 14: 4},
+        in_specs=smem + anywhere(12),
+        out_specs=tuple(anywhere(5)),
+        input_output_aliases={10: 0, 11: 1, 12: 2},
         scratch_shapes=[
             pltpu.VMEM((C, V), BF16), pltpu.VMEM((C, 2 * V), BF16), pltpu.VMEM((8, V), F32),
             pltpu.VMEM((27, V), jnp.int32), pltpu.VMEM((C, 27 * C), BF16), pltpu.VMEM((8 * C, C2), BF16),
             pltpu.VMEM((2 * VC, C2), BF16), pltpu.VMEM((CELLS, V), BF16), pltpu.VMEM((C, V), F32),
             pltpu.VMEM((C, V), BF16), pltpu.VMEM((C, V), F32), pltpu.VMEM((C, 28 * C), F32),
             pltpu.VMEM((8 * C, V), BF16), pltpu.VMEM((2 * VC, V), BF16),
-            pltpu.VMEM((ROWS_A, C2), F32), pltpu.VMEM((ROWS_B, C2), F32), pltpu.VMEM((VC, C2), F32),
-            pltpu.VMEM((VC, C2), BF16),
+            pltpu.VMEM(padded.shape, BF16), pltpu.VMEM((VC, C2), F32), pltpu.VMEM((VC, C2), BF16),
         ],
         compiler_params=pltpu.CompilerParams(vmem_limit_bytes=GRANT),
     )(
         wrong, feats, prev_f, next_f, table, neighbors, w_conv, w_down, grad_out, prev_g,
-        grad_pre, part_a, part_b, coarse_own, coarse_prev,
-    )
-
-    size_a, size_b = ROWS_A // (nx * ny), ROWS_B // (nx * ny)
-    most = max(nx, ny) - 1
+        sums, coarse_own, coarse_prev,
+    )
+
+    chunks, others = (nx * ny, CHUNK, C2), nx * ny - 1
     prev_p, next_p, coarse_out, grad_feats, done = pl.pallas_call(
         functools.partial(total_kernel, count, dims),
         name="total",
         out_shape=(
-            half, half, shape((VC, C2), BF16), shape((C, V), BF16), shape((nx, ny, 2, size_a, C2), BF16),
+            half, half, shape((VC, C2), BF16), shape((C, V), BF16), shape(chunks, BF16),
         ),
-        in_specs=vmem(10),
+        in_specs=smem + vmem(9),
         out_specs=tuple(vmem(5)),
         scratch_shapes=[
-            pltpu.VMEM((ny - 1, ROWS_A // ny, C2), F32), pltpu.VMEM((nx - 1, ROWS_B // nx, C2), F32),
-            pltpu.VMEM((nx, size_a, C2), F32), pltpu.VMEM((ny, size_b, C2), F32),
-            pltpu.VMEM((nx - 1, size_a, C2), F32), pltpu.VMEM((ny - 1, size_b, C2), F32),
-            pltpu.VMEM((nz, size_a + size_b, C2), F32), pltpu.VMEM((VC, C2), BF16),
+            pltpu.VMEM((others, CHUNK, C2), BF16), pltpu.VMEM((nz, CHUNK, C2), BF16),
+            pltpu.VMEM((VC, C2), BF16), pltpu.VMEM((C, V), BF16),
         ]
         + maps
         + [
             pltpu.VMEM((C, WIDE), BF16), pltpu.VMEM((TAPS, WIDE), BF16), pltpu.VMEM((TAPS, 3 * C), BF16),
             pltpu.VMEM((3 * C, WIDE), F32),
-            dma((3,)), dma((3,)), dma((2, most)), dma((2, most)), dma((2, most)), dma((2, most)),
-            dma((nz - 1,)), dma((nz - 1,)), dma((4, most)), dma((4, most)),
+            dma((3,)), dma((3,)), dma((others,)), dma((others,)), dma((nz - 1,)), dma((nz - 1,)),
+            dma((others,)), dma((others,)),
         ],
         compiler_params=pltpu.CompilerParams(
             collective_id=1, has_side_effects=True, vmem_limit_bytes=GRANT
         ),
     )(
-        grad_pre, slopes, back, coarse_own, coarse_prev, table, edges, weights,
-        part_a.reshape(ny, ROWS_A // ny, C2), part_b.reshape(nx, ROWS_B // nx, C2),
+        wrong, general, slopes, back, coarse_own, coarse_prev, table, edges, weights, sums.reshape(chunks),
     )
 
     coarse_out, grad_feats, grad_conv, grad_down = pl.pallas_call(
-        functools.partial(finish_kernel, dims, 1.0 / math.sqrt(V * count)),
+        functools.partial(finish_kernel, 1.0 / math.sqrt(V * count)),
         name="finish",
         out_shape=(
             shape((VC, C2), BF16), shape((C, V), BF16), shape((C, 27 * C), F32), shape((8 * C, C2), F32),
@@ -685,13 +642,14 @@
         in_specs=smem + vmem(3) + anywhere(6),
         out_specs=tuple(vmem(4)),
         scratch_shapes=[
-            pltpu.VMEM((ROWS_A + ROWS_B, C2), F32), pltpu.VMEM((C, 2 * V), BF16),
+            pltpu.VMEM((C, 2 * V), BF16),
             pltpu.VMEM((27, V), jnp.int32), pltpu.VMEM((C, 27 * C), BF16), pltpu.VMEM((C, V), F32),
             pltpu.VMEM((CELLS, V), BF16),
         ],
         compiler_params=pltpu.CompilerParams(vmem_limit_bytes=GRANT),
     )(
-        wrong, grad_feats, coarse_out, done, grad_pre, prev_p, next_p, neighbors, w_conv, back_general,
+        wrong, grad_feats, coarse_out, done.reshape(padded.shape), general, prev_p, next_p, neighbors, w_conv,
+        back_general,
     )
     return coarse_out, grad_feats.T, grad_conv.T, grad_down
 

time: 55.5 us -> 47.9 us (0.86)
  Pallas kernels: 54.6 us -> 47 us
    pallas_call x1, Pallas kernels: 33.1 us -> 26.1 us  [per_device(): pl.pallas_call(functools.partial(total_kernel, count, dims), name='total'...]
    pallas_call x1, Pallas kernels: 19 us -> 18.4 us  [per_device(): pl.pallas_call(functools.partial(block_kernel, count), name='block', out_...]
where the time goes in v4:
time: 47.9 us; the launch traced here: 47.7 us
  Pallas kernels  47 us (98%)
  between operations  0.66 us (1%)
    pallas_call x1, Pallas kernels, per_device(): pl.pallas_call(functools.partial(total_kernel, count, dims), name='total'...  26.1 us
    pallas_call x1, Pallas kernels, per_device(): pl.pallas_call(functools.partial(block_kernel, count), name='block', out_...  18.4 us
    pallas_call x1, Pallas kernels, per_device(): pl.pallas_call(functools.partial(finish_kernel, 1.0 / math.sqrt(V * count...  1.61 us

profile of v4, /device:TPU:8, one launch (start us, length us, event | category | flops | bytes accessed | tf_op | source)
XLA Modules:
  0.0 47.7 jit_solution(2391518670754853831)
XLA Ops:
  0.6 18.4 %block.1 = (bf16[64,2048]{1,0:T(8,128)(2,1)S(1)}, f32[64,2048]{1,0:T(8,128)S(1)}, bf16[1536,128]{1,0:T(8,128)(2,1)S(1)}, f32[256,128]{1,0:T(8,128)S(1)}, bf16[25...) custom-call(bf16[64,1024]{1,0:T(8,128)(2,1)} %bitcast.14, ...), custom_call_target="tpu_custom_call" | custom-call | tf_op jit(solution)/shard_map/block/pallas_call | solution.py:560
  19.0 0.0 copy-start
  19.0 0.8 %repair.1 = (bf16[1536,128]{1,0:T(8,128)(2,1)S(1)}, f32[256,128]{1,0:T(8,128)S(1)}, bf16[256,128]{1,0:T(8,128)(2,1)S(1)}, bf16[64,1024]{1,0:T(8,128)(2,1)S(1)}, f32[64,1024]{1,0:T(8,128)S(1)}) custom-call(f32[1]{0:T(128)} %get-tuple-element.29.wrong, bf16[64,1024]{1,0:T(8,128)(2,1)} %bitcast.15, ...), custom_call_target="tpu_custom_call", output_to_operand_aliasing={{0}: (10, {}), {1}: (11, {}), {2}: (12, {})} | custom-call | tf_op jit(solution)/shard_map/repair/pallas_call | solution.py:586
  19.9 0.1 copy-done
  20.0 26.1 %total.1 = (bf16[64,512]{1,0:T(8,128)(2,1)S(1)}, bf16[64,512]{1,0:T(8,128)(2,1)S(1)}, bf16[256,128]{1,0:T(8,128)(2,1)S(1)}, bf16[64,1024]{1,0:T(8,128)(2,1)S(1)}, bf16[16,96,128]{2,1,0:T(8,128)(2,1)S(1)}) custom-call(f32[1]{0:T(128)} %get-tuple-element.29.wrong, bf16[64,1024]{1,0:T(8,128)(2,1)S(1)} %get-tuple-element.37.general.grad_pre, ...), custom_call_target="tpu_custom_call" | custom-call | tf_op jit(solution)/shard_map/total/pallas_call | solution.py:610
  46.1 1.6 %finish.1 = (bf16[256,128]{1,0:T(8,128)(2,1)}, bf16[64,1024]{1,0:T(8,128)(2,1)}, f32[64,1728]{1,0:T(8,128)}, f32[512,128]{1,0:T(8,128)}) custom-call(f32[1]{0:T(128)} %get-tuple-element.29.wrong, bf16[64,1024]{1,0:T(8,128)(2,1)S(1)} %get-tuple-element.44.grad_fast, bf16[256,128]{1,0:T(8,128)(2,1)S(1)} %get-tuple-element.45.coarse, ...), custom_call_target="tpu_custom_call" | custom-call | tf_op jit(solution)/shard_map/finish/pallas_call | solution.py:636
Async XLA Ops:
  19.0 0.9 %copy-start = (bf16[1728,64]{0,1:T(8,128)(2,1)S(1)}, bf16[1728,64]{0,1:T(8,128)(2,1)}, u32[]{:S(2)}) copy-start(bf16[1728,64]{0,1:T(8,128)(2,1)} %param.8) | copy-start | bytes 663556
